TPU v7x, 128 devices: a whole 4x4x4 slice. The times are simulated.
128 devices in a mesh: dp: 4 (over x_hi, core), ctx: 32 (over z, y, x_lo).
Axes of the slice: x: 4 (x_hi: 2, x_lo: 2; x = x_hi * 2 + x_lo), y: 4, z: 4, core: 2. Of those that a mesh axis runs over, the one named last changes fastest.
Arguments:
- gate_input: bfloat16 [4, 4096, 4096], P('dp', 'ctx'), may hold values from -6 to 6
- values: bfloat16 [4, 4096, 4096], P('dp', 'ctx'), may hold values from -6 to 6
- cotangent: bfloat16 [4, 4096, 4096], P('dp', 'ctx'), may hold values from -6 to 6
- filter_taps: float32 [4096, 4096], P(('dp', 'ctx')), may hold values from -4 to 4
Outputs:
- output: bfloat16 [4, 4096, 4096], P('dp', 'ctx')
- gate_grad: bfloat16 [4, 4096, 4096], P('dp', 'ctx')
- values_grad: bfloat16 [4, 4096, 4096], P('dp', 'ctx')
- filter_grad: float32 [4096, 4096], P(('dp', 'ctx'))
All inputs are finite; a program needn't handle non-finite values.
Results may differ from a plain program's by a relative error of at most 0.013.
Values may be sent and summed in bfloat16 or wider, within the bound.
No kernel may reach another device: no remote copies, remote signals or barrier semaphores. Data moves between devices by JAX's collectives and lax.ppermute only.
A program may use at most 128 MiB of HBM per device.

v0:
```python
import functools
import math

import jax
import jax.numpy as jnp
import ml_dtypes
import numpy as np
from jax import lax
from jax.experimental import pallas as pl
from jax.experimental.pallas import tpu as pltpu
from jax.sharding import PartitionSpec as P

LANES = 128
PACK = 16
BF16 = jnp.bfloat16
F32 = jnp.float32


def angle_tables(top, bottom, period):
    angles = (np.outer(top, bottom) % period).astype(np.float64) * (2.0 * math.pi / period)
    return np.cos(angles).astype(np.float32), np.sin(angles).astype(np.float32)


def block_diagonal(table):
    eye = np.eye(PACK, dtype=np.float32)
    return np.kron(table, eye).astype(ml_dtypes.bfloat16)


def dft_tables(blocks):
    freq_len = blocks * LANES
    half = blocks // 2
    cosine, sine = angle_tables(np.arange(blocks), np.arange(half), blocks)
    first = np.zeros((blocks, half), np.float32)
    first[0] = cosine[0]
    first[1] = cosine[half]
    for p in range(1, half):
        first[2 * p] = cosine[p]
        first[2 * p + 1] = -sine[p]
    weight = np.full((blocks,), 2.0 / freq_len, np.float32)
    weight[:2] = 1.0 / freq_len
    last = (first * weight[:, None]).T
    twist_cosine, twist_sine = angle_tables(np.arange(half + 1), np.arange(LANES), freq_len)
    inner_cosine, inner_sine = angle_tables(np.arange(LANES), np.arange(LANES), LANES)
    forward = np.block([[inner_cosine, -inner_sine], [inner_sine, inner_cosine]])
    inverse = np.block([[inner_cosine, inner_sine], [-inner_sine, inner_cosine]])
    return (
        block_diagonal(first),
        block_diagonal(last),
        twist_cosine[:, None, :],
        twist_sine[:, None, :],
        forward.astype(ml_dtypes.bfloat16),
        inverse.astype(ml_dtypes.bfloat16),
    )


def swap_lane_groups(pieces):
    count = len(pieces)
    width = LANES // count
    group = lax.broadcasted_iota(jnp.int32, pieces[0].shape, pieces[0].ndim - 1) // width
    results = []
    for g in range(count):
        total = None
        for k in range(count):
            shift = (width * (k - g)) % LANES
            moved = pieces[k] if shift == 0 else pltpu.roll(pieces[k], shift, pieces[k].ndim - 1)
            total = moved if total is None else jnp.where(group == k, moved, total)
        results.append(total)
    return results


def pack_kernel(gate_ref, values_ref, cotangent_ref, taps_ref, packed_ref):
    columns = values_ref.shape[-1]
    per_peer = 32
    peers = columns // per_peer
    flipped = values_ref[0].T
    packed_ref[:, 0:per_peer, :] = flipped.reshape(peers, per_peer, LANES)
    grad = (cotangent_ref[0].astype(F32) * gate_ref[0].astype(F32)).astype(BF16)
    packed_ref[:, per_peer : 2 * per_peer, :] = grad.T.reshape(peers, per_peer, LANES)
    taps = taps_ref[...]
    stacked = jnp.concatenate([taps[:, LANES * n : LANES * (n + 1)] for n in range(4)], axis=0)
    turned = stacked.T.reshape(4, 4, 8, LANES)
    pieces = swap_lane_groups([turned[:, k] for k in range(4)])
    for n in range(4):
        packed_ref[4 * n : 4 * n + 4, 2 * per_peer : 2 * per_peer + 8, :] = pieces[n].astype(BF16)


def unpack_kernel(gate_ref, cotangent_ref, packed_ref, output_ref, gate_grad_ref, values_grad_ref, taps_ref):
    columns = output_ref.shape[-1]
    per_peer = 32
    conv = packed_ref[:, 0:per_peer, :].reshape(columns, LANES).T.astype(F32)
    output_ref[0] = (gate_ref[0].astype(F32) * conv).astype(BF16)
    gate_grad_ref[0] = (cotangent_ref[0].astype(F32) * conv).astype(BF16)
    values_grad_ref[0] = packed_ref[:, per_peer : 2 * per_peer, :].reshape(columns, LANES).T
    taps = packed_ref[:, 2 * per_peer : 2 * per_peer + 8, :].astype(F32)
    pieces = swap_lane_groups([taps[4 * n : 4 * n + 4] for n in range(4)])
    stacked = jnp.stack(pieces, axis=1).reshape(LANES, LANES).T
    for n in range(4):
        taps_ref[:, LANES * n : LANES * (n + 1)] = stacked[32 * n : 32 * n + 32, :]


def conv_kernel(
    data_ref, first_ref, last_ref, cosine_ref, sine_ref, forward_ref, inverse_ref, out_ref,
    filter_ref, twisted_ref, mixed_ref,
):
    half = 32
    rows = twisted_ref.shape[1]

    taps = data_ref[:, 64:72, :].astype(F32).reshape(half, 4, 8, LANES)
    pieces = swap_lane_groups([taps[:, m] for m in range(4)])
    for k in range(4):
        filter_ref[:, 8 * k : 8 * k + 8, :] = pieces[k]

    def first_section(left, right, row):
        both = jnp.concatenate([left.reshape(half * PACK, LANES), right.reshape(half * PACK, LANES)], axis=1)
        rows_out = jnp.dot(first_ref[...], both, preferred_element_type=F32)
        for p in range(half + 1):
            for side in range(2):
                lanes = slice(LANES * side, LANES * (side + 1))
                target = pl.ds(row + PACK * side, PACK)
                if p == 0:
                    real = rows_out[0:PACK, lanes]
                    imag = jnp.zeros((PACK, LANES), F32)
                elif p == half:
                    part = rows_out[PACK : 2 * PACK, lanes]
                    real = part * cosine_ref[p]
                    imag = -part * sine_ref[p]
                else:
                    start = 2 * p * PACK
                    first = rows_out[start : start + PACK, lanes]
                    second = rows_out[start + PACK : start + 2 * PACK, lanes]
                    real = first * cosine_ref[p] + second * sine_ref[p]
                    imag = second * cosine_ref[p] - first * sine_ref[p]
                twisted_ref[p, target, 0:LANES] = real.astype(BF16)
                twisted_ref[p, target, LANES : 2 * LANES] = imag.astype(BF16)

    def signal_step(t, carry):
        kind = t // 4
        member = t % 4
        places = pl.ds(pl.multiple_of(member * half, half), half)
        column = pl.multiple_of(kind * half, half)
        left = data_ref[places, pl.ds(column, PACK), :]
        right = data_ref[places, pl.ds(column + PACK, PACK), :]
        first_section(left, right, pl.multiple_of(t * half, half))
        return carry

    lax.fori_loop(0, 8, signal_step, 0)
    first_section(
        filter_ref[:, 0:PACK, :].astype(BF16), filter_ref[:, PACK : 2 * PACK, :].astype(BF16), 256
    )

    def spectrum_step(p):
        spec = jnp.dot(twisted_ref[p], forward_ref[...], preferred_element_type=F32)
        filter_r, filter_i = spec[256:288, 0:LANES], spec[256:288, LANES:]
        conv_r, conv_i, back_r, back_i = [], [], [], []
        taps_r = taps_i = None
        for d in range(4):
            at = slice(32 * d, 32 * d + 32)
            value_r, value_i = spec[at, 0:LANES], spec[at, LANES:]
            at = slice(128 + 32 * d, 128 + 32 * d + 32)
            grad_r, grad_i = spec[at, 0:LANES], spec[at, LANES:]
            conv_r.append((value_r * filter_r - value_i * filter_i).astype(BF16))
            conv_i.append((value_r * filter_i + value_i * filter_r).astype(BF16))
            back_r.append((grad_r * filter_r + grad_i * filter_i).astype(BF16))
            back_i.append((grad_i * filter_r - grad_r * filter_i).astype(BF16))
            part_r = grad_r * value_r + grad_i * value_i
            part_i = grad_i * value_r - grad_r * value_i
            taps_r = part_r if d == 0 else taps_r + part_r
            taps_i = part_i if d == 0 else taps_i + part_i
        real = jnp.concatenate(conv_r + back_r + [taps_r.astype(BF16)], axis=0)
        imag = jnp.concatenate(conv_i + back_i + [taps_i.astype(BF16)], axis=0)
        mixture = jnp.dot(
            jnp.concatenate([real, imag], axis=1), inverse_ref[...], preferred_element_type=F32
        )
        first, second = mixture[:, 0:LANES], mixture[:, LANES:]
        at_r = jnp.where(p == half, 1, 2 * p)
        at_i = jnp.where(p == 0, 2 * half, jnp.where(p == half, 2 * half + 1, 2 * p + 1))
        mixed_ref[at_r] = (first * cosine_ref[p] - second * sine_ref[p]).astype(BF16)
        mixed_ref[at_i] = (second * cosine_ref[p] + first * sine_ref[p]).astype(BF16)

    def spectrum_group(n, carry):
        for m in range(3):
            spectrum_step(3 * n + m)
        return carry

    lax.fori_loop(0, (half + 1) // 3, spectrum_group, 0)

    def last_section(row):
        left = mixed_ref[0 : 2 * half, pl.ds(row, PACK), :].reshape(2 * half * PACK, LANES)
        right = mixed_ref[0 : 2 * half, pl.ds(row + PACK, PACK), :].reshape(2 * half * PACK, LANES)
        both = jnp.concatenate([left, right], axis=1)
        return jnp.dot(last_ref[...], both, preferred_element_type=F32)

    def inverse_step(t, carry):
        kind = t // 4
        member = t % 4
        places = pl.ds(pl.multiple_of(member * half, half), half)
        column = pl.multiple_of(kind * half, half)
        result = last_section(pl.multiple_of(t * half, half)).astype(BF16)
        out_ref[places, pl.ds(column, PACK), :] = result[:, 0:LANES].reshape(half, PACK, LANES)
        out_ref[places, pl.ds(column + PACK, PACK), :] = result[:, LANES:].reshape(half, PACK, LANES)
        return carry

    lax.fori_loop(0, 8, inverse_step, 0)
    result = last_section(256)
    filter_ref[:, 0:PACK, :] = result[:, 0:LANES].reshape(half, PACK, LANES)
    filter_ref[:, PACK : 2 * PACK, :] = result[:, LANES:].reshape(half, PACK, LANES)
    pieces = swap_lane_groups([filter_ref[:, 8 * k : 8 * k + 8, :] for k in range(4)])
    stacked = jnp.stack(pieces, axis=1).reshape(4 * half, 8, LANES)
    out_ref[:, 64:72, :] = stacked.astype(BF16)


def on_device(tables, gate_input, values, cotangent, filter_taps):
    channels = values.shape[2]
    peers = lax.axis_size("dp") * lax.axis_size("ctx")
    width = 512
    steps = channels // width
    limit = pltpu.CompilerParams(vmem_limit_bytes=48 * 1024 * 1024)
    wide = pl.BlockSpec((1, LANES, width), lambda n: (0, 0, n))
    taps_block = pl.BlockSpec((32, width), lambda n: (0, n))
    packed_block = pl.BlockSpec((width // 32, 72, LANES), lambda n: (n, 0, 0))
    packed_shape = jax.ShapeDtypeStruct((peers, 72, LANES), BF16)
    packed = pl.pallas_call(
        pack_kernel,
        grid=(steps,),
        in_specs=[wide, wide, wide, taps_block],
        out_specs=packed_block,
        out_shape=packed_shape,
        compiler_params=limit,
        name="pack",
    )(gate_input, values, cotangent, filter_taps)
    received = lax.all_to_all(packed, ("dp", "ctx"), split_axis=0, concat_axis=0, tiled=True)
    whole = pl.BlockSpec(memory_space=pltpu.VMEM)
    results = pl.pallas_call(
        conv_kernel,
        in_specs=[whole] * 7,
        out_specs=whole,
        out_shape=packed_shape,
        scratch_shapes=[
            pltpu.VMEM((32, 32, LANES), F32),
            pltpu.VMEM((33, 288, 2 * LANES), BF16),
            pltpu.VMEM((66, 288, LANES), BF16),
        ],
        compiler_params=limit,
        name="convolve",
    )(received, *tables)
    returned = lax.all_to_all(results, ("dp", "ctx"), split_axis=0, concat_axis=0, tiled=True)
    wide_shape = jax.ShapeDtypeStruct(values.shape, BF16)
    return pl.pallas_call(
        unpack_kernel,
        grid=(steps,),
        in_specs=[wide, wide, packed_block],
        out_specs=[wide, wide, wide, taps_block],
        out_shape=[wide_shape, wide_shape, wide_shape, jax.ShapeDtypeStruct(filter_taps.shape, F32)],
        compiler_params=limit,
        name="unpack",
    )(gate_input, cotangent, returned)


def solution(mesh):
    tables = dft_tables(64)
    specs = (
        P("dp", "ctx", None),
        P("dp", "ctx", None),
        P("dp", "ctx", None),
        P(("dp", "ctx"), None),
    )

    def program(gate_input, values, cotangent, filter_taps):
        body = functools.partial(on_device, tables)
        return jax.shard_map(
            lambda *args: tuple(body(*args)), mesh=mesh, in_specs=specs, out_specs=specs, check_vma=False
        )(gate_input, values, cotangent, filter_taps)

    return program
```

profile of v0, /device:TPU:1, one launch (start us, length us, event | category | flops | bytes accessed | tf_op | source)
XLA Modules:
  0.0 110.8 jit_solution(10168177288530480322)
XLA Ops:
  0.6 0.0 copy-start
  0.6 1.2 %copy-done = bf16[1,128,4096]{2,1,0:T(8,128)(2,1)S(1)} copy-done((bf16[1,128,4096]{2,1,0:T(8,128)(2,1)S(1)}, bf16[1,128,4096]{2,1,0:T(8,128)(2,1)}, u32[]{:S(2)}) %copy-start) | copy-done | bytes 1048600
  1.9 0.0 copy-start.2
  1.9 1.2 %copy-done.2 = bf16[1,128,4096]{2,1,0:T(8,128)(2,1)S(1)} copy-done((bf16[1,128,4096]{2,1,0:T(8,128)(2,1)S(1)}, bf16[1,128,4096]{2,1,0:T(8,128)(2,1)}, u32[]{:S(2)}) %copy-start.2) | copy-done | bytes 1048600
  3.1 0.0 copy-start.4
  3.1 1.2 %copy-done.4 = bf16[1,128,4096]{2,1,0:T(8,128)(2,1)S(1)} copy-done((bf16[1,128,4096]{2,1,0:T(8,128)(2,1)S(1)}, bf16[1,128,4096]{2,1,0:T(8,128)(2,1)}, u32[]{:S(2)}) %copy-start.4) | copy-done | bytes 1048600
  4.3 0.0 copy-start.7
  4.3 1.0 copy-done.7
  5.4 2.5 %pack.1 = bf16[128,72,128]{2,1,0:T(8,128)(2,1)S(1)} custom-call(bf16[1,128,4096]{2,1,0:T(8,128)(2,1)S(1)} %copy-done, bf16[1,128,4096]{2,1,0:T(8,128)(2,1)S(1)} %copy-done.4, bf16[1,128,4096]{2,1,0:T(8,128)(2,1)S(1)} %copy-done.2, f32[32,4096]{1,0:T(8,128)S(1)} %copy-done.7), custom_call_target="tpu_custom_call" | custom-call | tf_op jit(solution)/shard_map/pack/pallas_call | solution.py:222
  7.8 0.0 copy-start.5
  7.9 0.0 copy-start.6
  7.9 0.0 copy-start.8
  7.9 0.0 copy-start.9
  7.9 0.0 copy-start.10
  7.9 0.0 copy-start.11
  7.9 44.8 %all_to_all.10.data_ref = bf16[128,72,128]{2,1,0:T(8,128)(2,1)} all-to-all(bf16[128,72,128]{2,1,0:T(8,128)(2,1)S(1)} %pack.1), channel_id=1, replica_groups=mesh['dp'=4,'ctx'=32] {'dp','ctx'}, dimensions={0} | all-to-all | bytes 4718592 | tf_op jit(solution)/shard_map/all_to_all | solution.py:231
  52.7 0.0 copy-done.5
  52.7 0.0 copy-done.6
  52.7 0.0 copy-done.8
  52.8 0.0 copy-done.9
  52.8 0.0 copy-done.10
  52.8 0.0 copy-done.11
  52.8 16.7 %convolve.1 = bf16[128,72,128]{2,1,0:T(8,128)(2,1)S(1)} custom-call(bf16[128,72,128]{2,1,0:T(8,128)(2,1)} %all_to_all.10.data_ref, bf16[1024,512]{1,0:T(8,128)(2,1)S(1)} %copy-done.6, bf16[512,1024]{1,0:T(8,128)(2,1)S(1)} %copy-done.5, f32[33,1,128]{2,1,0:T(1,128)S(1)} %copy-done.11, f32[33,1,128]{2,1,0:T(1,128)S(1)} %copy-done.10, ...), custom_call_target="tpu_custom_call" | custom-call | tf_op jit(solution)/shard_map/convolve/pallas_call | solution.py:233
  69.4 0.0 copy-start.1
  69.5 0.0 copy-start.3
  69.5 37.4 %all_to_all.11.packed_ref = bf16[128,72,128]{2,1,0:T(8,128)(2,1)S(1)} all-to-all(bf16[128,72,128]{2,1,0:T(8,128)(2,1)S(1)} %convolve.1), channel_id=1, replica_groups=mesh['dp'=4,'ctx'=32] {'dp','ctx'}, dimensions={0} | all-to-all | bytes 4718592 | tf_op jit(solution)/shard_map/all_to_all | solution.py:246
  106.8 0.0 copy-done.1
  106.8 0.0 copy-done.3
  106.8 4.0 %unpack.1 = (bf16[1,128,4096]{2,1,0:T(8,128)(2,1)}, bf16[1,128,4096]{2,1,0:T(8,128)(2,1)}, bf16[1,128,4096]{2,1,0:T(8,128)(2,1)}, f32[32,4096]{1,0:T(8,128)}) custom-call(bf16[1,128,4096]{2,1,0:T(8,128)(2,1)S(1)} %copy-done.1, bf16[1,128,4096]{2,1,0:T(8,128)(2,1)S(1)} %copy-done.3, bf16[128,72,128]{2,1,0:T(8,128)(2,1)S(1)} %all_to_all.11.packed_ref), custom_call_target="tpu_custom_call" | custom-call | tf_op jit(solution)/shard_map/unpack/pallas_call | solution.py:248
Async XLA Ops:
  0.6 1.2 %copy-start = (bf16[1,128,4096]{2,1,0:T(8,128)(2,1)S(1)}, bf16[1,128,4096]{2,1,0:T(8,128)(2,1)}, u32[]{:S(2)}) copy-start(bf16[1,128,4096]{2,1,0:T(8,128)(2,1)} %gate_ref.3) | copy-start | bytes 3145732
  1.9 1.2 %copy-start.2 = (bf16[1,128,4096]{2,1,0:T(8,128)(2,1)S(1)}, bf16[1,128,4096]{2,1,0:T(8,128)(2,1)}, u32[]{:S(2)}) copy-start(bf16[1,128,4096]{2,1,0:T(8,128)(2,1)} %cotangent_ref.3) | copy-start | bytes 3145732
  3.1 1.2 %copy-start.4 = (bf16[1,128,4096]{2,1,0:T(8,128)(2,1)S(1)}, bf16[1,128,4096]{2,1,0:T(8,128)(2,1)}, u32[]{:S(2)}) copy-start(bf16[1,128,4096]{2,1,0:T(8,128)(2,1)} %values_ref.1) | copy-start | bytes 3145732
  4.3 1.0 copy-start.7
  7.8 44.9 %copy-start.5 = (bf16[512,1024]{1,0:T(8,128)(2,1)S(1)}, bf16[512,1024]{1,0:T(8,128)(2,1)}, u32[]{:S(2)}) copy-start(bf16[512,1024]{1,0:T(8,128)(2,1)} %constant.13.clone.last_ref) | copy-start | bytes 3145732
  7.9 44.9 %copy-start.6 = (bf16[1024,512]{1,0:T(8,128)(2,1)S(1)}, bf16[1024,512]{1,0:T(8,128)(2,1)}, u32[]{:S(2)}) copy-start(bf16[1024,512]{1,0:T(8,128)(2,1)} %constant.12.clone.first_ref) | copy-start | bytes 3145732
  7.9 44.9 %copy-start.8 = (bf16[256,256]{1,0:T(8,128)(2,1)S(1)}, bf16[256,256]{1,0:T(8,128)(2,1)}, u32[]{:S(2)}) copy-start(bf16[256,256]{1,0:T(8,128)(2,1)} %constant.17.clone.inverse_ref) | copy-start | bytes 393220
  7.9 44.9 %copy-start.9 = (bf16[256,256]{1,0:T(8,128)(2,1)S(1)}, bf16[256,256]{1,0:T(8,128)(2,1)}, u32[]{:S(2)}) copy-start(bf16[256,256]{1,0:T(8,128)(2,1)} %constant.16.clone.forward_ref) | copy-start | bytes 393220
  7.9 44.9 %copy-start.10 = (f32[33,1,128]{2,1,0:T(1,128)S(1)}, f32[33,1,128]{2,1,0:T(1,128)}, u32[]{:S(2)}) copy-start(f32[33,1,128]{2,1,0:T(1,128)} %constant.15.clone.sine_ref) | copy-start | bytes 50692
  7.9 44.9 %copy-start.11 = (f32[33,1,128]{2,1,0:T(1,128)S(1)}, f32[33,1,128]{2,1,0:T(1,128)}, u32[]{:S(2)}) copy-start(f32[33,1,128]{2,1,0:T(1,128)} %constant.14.clone.cosine_ref) | copy-start | bytes 50692
  69.4 37.4 %copy-start.1 = (bf16[1,128,4096]{2,1,0:T(8,128)(2,1)S(1)}, bf16[1,128,4096]{2,1,0:T(8,128)(2,1)}, u32[]{:S(2)}) copy-start(bf16[1,128,4096]{2,1,0:T(8,128)(2,1)} %gate_ref.3) | copy-start | bytes 3145732
  69.5 37.4 %copy-start.3 = (bf16[1,128,4096]{2,1,0:T(8,128)(2,1)S(1)}, bf16[1,128,4096]{2,1,0:T(8,128)(2,1)}, u32[]{:S(2)}) copy-start(bf16[1,128,4096]{2,1,0:T(8,128)(2,1)} %cotangent_ref.3) | copy-start | bytes 3145732
where the time goes:
time: 111 us
  blocking collectives  82.2 us (74%)
  Pallas kernels  23.1 us (21%)
  local copies, waits for them, and re-layouts  4.76 us (4%)
    all_to_all x1, blocking collectives, on_device(): lax.all_to_all(packed, ('dp', 'ctx'), split_axis=0, concat_axis=0, tiled=...  44.8 us
    all_to_all x1, blocking collectives, on_device(): lax.all_to_all(results, ('dp', 'ctx'), split_axis=0, concat_axis=0, tiled...  37.4 us
    pallas_call x1, Pallas kernels, on_device(): pl.pallas_call(conv_kernel, in_specs=[whole] * 7, out_specs=whole, out_sh...  16.7 us
    unnamed x24, local copies, waits for them, and re-layouts  4.76 us
    pallas_call x1, Pallas kernels, on_device(): pl.pallas_call(unpack_kernel, grid=(steps,), in_specs=[wide, wide, packed...  3.97 us
    pallas_call x1, Pallas kernels, on_device(): pl.pallas_call(pack_kernel, grid=(steps,), in_specs=[wide, wide, wide, ta...  2.49 us

commit v1 on v0

v1 whole, which is shorter than its diff:
```python
import functools
import math

import jax
import jax.numpy as jnp
import ml_dtypes
import numpy as np
from jax import lax
from jax.experimental import pallas as pl
from jax.experimental.pallas import tpu as pltpu
from jax.sharding import PartitionSpec as P

LANES = 128
PACK = 16
PACK_LIMIT = 16 * 1024 * 1024
CONV_LIMIT = 32 * 1024 * 1024
BF16 = jnp.bfloat16
F32 = jnp.float32


def angle_tables(top, bottom, period):
    angles = (np.outer(top, bottom) % period).astype(np.float64) * (2.0 * math.pi / period)
    return np.cos(angles).astype(np.float32), np.sin(angles).astype(np.float32)


def block_diagonal(table):
    eye = np.eye(PACK, dtype=np.float32)
    return np.kron(table, eye).astype(ml_dtypes.bfloat16)


def dft_tables(blocks):
    freq_len = blocks * LANES
    half = blocks // 2
    quarter = half // 2
    firsts, lasts = [], []
    for parity in range(2):
        places = np.arange(parity, half, 2)
        cosine, sine = angle_tables(np.arange(quarter + 1), places, blocks)
        base = np.zeros((half, quarter), np.float32)
        base[0] = cosine[0]
        base[1] = cosine[quarter] if parity == 0 else -sine[quarter]
        for p in range(1, quarter):
            base[2 * p] = cosine[p]
            base[2 * p + 1] = -sine[p]
        weight = np.full((half, 1), 2.0 / freq_len, np.float32)
        weight[0] = 1.0 / freq_len
        firsts.append(block_diagonal(base))
        lasts.append(block_diagonal((base * weight).T))
    order = [p for u in range(quarter) for p in (u, half - u)] + [quarter]
    twist_cosine, twist_sine = angle_tables(np.array(order), np.arange(LANES), freq_len)
    inner_cosine, inner_sine = angle_tables(np.arange(LANES), np.arange(LANES), LANES)
    forward = np.block([[inner_cosine, -inner_sine], [inner_sine, inner_cosine]])
    inverse = np.block([[inner_cosine, inner_sine], [-inner_sine, inner_cosine]])
    return (
        np.stack(firsts),
        np.stack(lasts),
        twist_cosine[:, None, :],
        twist_sine[:, None, :],
        forward.astype(ml_dtypes.bfloat16),
        inverse.astype(ml_dtypes.bfloat16),
    )


def swap_lane_groups(pieces):
    count = len(pieces)
    width = LANES // count
    group = lax.broadcasted_iota(jnp.int32, pieces[0].shape, pieces[0].ndim - 1) // width
    results = []
    for g in range(count):
        total = None
        for k in range(count):
            shift = (width * (k - g)) % LANES
            moved = pieces[k] if shift == 0 else pltpu.roll(pieces[k], shift, pieces[k].ndim - 1)
            total = moved if total is None else jnp.where(group == k, moved, total)
        results.append(total)
    return results


def in_place(array):
    return pltpu.with_memory_space_constraint(array, pltpu.HBM)


def pack_kernel(
    gate_any, values_any, cotangent_any, taps_any, packed_ref,
    gate_ref, values_ref, cotangent_ref, taps_ref, arrived,
):
    pairs = (
        (values_any, values_ref),
        (cotangent_any, cotangent_ref),
        (gate_any, gate_ref),
        (taps_any, taps_ref),
    )
    chunks = arrived.shape[1]
    columns = taps_ref.shape[-1] // chunks
    per_peer = 32
    peers = columns // per_peer

    def copy(n, m):
        source, target = pairs[m]
        at = slice(n * columns, (n + 1) * columns)
        if m == 3:
            return pltpu.make_async_copy(source.at[:, at], target.at[:, at], arrived.at[m, n])
        return pltpu.make_async_copy(source.at[0, :, at], target.at[:, at], arrived.at[m, n])

    for n in range(chunks):
        for m in range(4):
            copy(n, m).start()
    for n in range(chunks):
        at = slice(n * columns, (n + 1) * columns)
        to = slice(n * peers, (n + 1) * peers)
        copy(n, 0).wait()
        packed_ref[to, 0:per_peer, :] = values_ref[:, at].T.reshape(peers, per_peer, LANES)
        copy(n, 1).wait()
        copy(n, 2).wait()
        grad = (cotangent_ref[:, at].astype(F32) * gate_ref[:, at].astype(F32)).astype(BF16)
        packed_ref[to, per_peer : 2 * per_peer, :] = grad.T.reshape(peers, per_peer, LANES)
        copy(n, 3).wait()
        taps = taps_ref[:, at]
        for block in range(columns // 512):
            start = 512 * block
            stacked = jnp.concatenate(
                [taps[:, start + LANES * i : start + LANES * (i + 1)] for i in range(4)], axis=0
            )
            turned = stacked.T.reshape(4, 4, 8, LANES)
            pieces = swap_lane_groups([turned[:, k] for k in range(4)])
            for i in range(4):
                first = n * peers + 16 * block + 4 * i
                packed_ref[first : first + 4, 2 * per_peer : 2 * per_peer + 8, :] = pieces[i].astype(BF16)


def pack(gate_input, values, cotangent, filter_taps):
    channels = values.shape[2]
    chunks = 4
    anywhere = pl.BlockSpec(memory_space=pltpu.HBM)
    return pl.pallas_call(
        pack_kernel,
        in_specs=[anywhere] * 4,
        out_specs=pl.BlockSpec(memory_space=pltpu.VMEM),
        out_shape=jax.ShapeDtypeStruct((channels // 32, 72, LANES), BF16),
        scratch_shapes=[
            pltpu.VMEM((LANES, channels), BF16),
            pltpu.VMEM((LANES, channels), BF16),
            pltpu.VMEM((LANES, channels), BF16),
            pltpu.VMEM((32, channels), F32),
            pltpu.SemaphoreType.DMA((4, chunks)),
        ],
        compiler_params=pltpu.CompilerParams(vmem_limit_bytes=PACK_LIMIT),
        name="pack",
    )(*[in_place(x) for x in (gate_input, values, cotangent, filter_taps)])


def unpack_kernel(
    gate_any, cotangent_any, packed_ref, output_any, gate_grad_any, values_grad_any, taps_any,
    gate_ref, cotangent_ref, output_ref, gate_grad_ref, values_grad_ref, taps_ref, arrived, left,
):
    pairs = (
        (values_grad_ref, values_grad_any),
        (output_ref, output_any),
        (gate_grad_ref, gate_grad_any),
        (taps_ref, taps_any),
    )
    chunks = left.shape[1]
    columns = taps_ref.shape[-1] // chunks
    per_peer = 32
    peers = columns // per_peer

    def copy(n, m):
        source, target = pairs[m]
        at = slice(n * columns, (n + 1) * columns)
        if m == 3:
            return pltpu.make_async_copy(source.at[:, at], target.at[:, at], left.at[m, n])
        return pltpu.make_async_copy(source.at[:, at], target.at[0, :, at], left.at[m, n])

    def fetch(n, m):
        at = slice(n * columns, (n + 1) * columns)
        source, target = ((gate_any, gate_ref), (cotangent_any, cotangent_ref))[m]
        return pltpu.make_async_copy(source.at[0, :, at], target.at[:, at], arrived.at[m, n])

    for n in range(chunks):
        for m in range(2):
            fetch(n, m).start()
    for n in range(chunks):
        at = slice(n * columns, (n + 1) * columns)
        of = slice(n * peers, (n + 1) * peers)
        values_grad_ref[:, at] = packed_ref[of, per_peer : 2 * per_peer, :].reshape(columns, LANES).T
        copy(n, 0).start()
        taps = packed_ref[of, 2 * per_peer : 2 * per_peer + 8, :].astype(F32)
        for block in range(columns // 512):
            pieces = swap_lane_groups(
                [taps[16 * block + 4 * i : 16 * block + 4 * i + 4] for i in range(4)]
            )
            stacked = jnp.stack(pieces, axis=1).reshape(LANES, LANES).T
            for i in range(4):
                start = n * columns + 512 * block + LANES * i
                taps_ref[:, start : start + LANES] = stacked[32 * i : 32 * i + 32, :]
        copy(n, 3).start()
    for n in range(chunks):
        at = slice(n * columns, (n + 1) * columns)
        of = slice(n * peers, (n + 1) * peers)
        conv = packed_ref[of, 0:per_peer, :].reshape(columns, LANES).T.astype(F32)
        fetch(n, 0).wait()
        output_ref[:, at] = (gate_ref[:, at].astype(F32) * conv).astype(BF16)
        copy(n, 1).start()
        fetch(n, 1).wait()
        gate_grad_ref[:, at] = (cotangent_ref[:, at].astype(F32) * conv).astype(BF16)
        copy(n, 2).start()
    for n in range(chunks):
        for m in range(4):
            copy(n, m).wait()


def unpack(gate_input, cotangent, packed):
    channels = gate_input.shape[2]
    chunks = 4
    within = pl.BlockSpec(memory_space=pltpu.VMEM)
    outside = pl.BlockSpec(memory_space=pltpu.HBM)
    wide_shape = jax.ShapeDtypeStruct(gate_input.shape, BF16)
    return pl.pallas_call(
        unpack_kernel,
        in_specs=[outside, outside, within],
        out_specs=[outside] * 4,
        out_shape=[wide_shape, wide_shape, wide_shape, jax.ShapeDtypeStruct((32, channels), F32)],
        scratch_shapes=[
            pltpu.VMEM((LANES, channels), BF16),
            pltpu.VMEM((LANES, channels), BF16),
            pltpu.VMEM((LANES, channels), BF16),
            pltpu.VMEM((LANES, channels), BF16),
            pltpu.VMEM((LANES, channels), BF16),
            pltpu.VMEM((32, channels), F32),
            pltpu.SemaphoreType.DMA((2, chunks)),
            pltpu.SemaphoreType.DMA((4, chunks)),
        ],
        compiler_params=pltpu.CompilerParams(vmem_limit_bytes=PACK_LIMIT),
        name="unpack",
    )(in_place(gate_input), in_place(cotangent), packed)


def conv_kernel(
    data_ref, first_ref, last_ref, cosine_ref, sine_ref, forward_ref, inverse_ref, out_ref,
    filter_ref, twisted_ref, mixed_ref,
):
    half = 32
    quarter = 16
    rows = 288

    taps = data_ref[:, 64:72, :].astype(F32).reshape(half, 4, 8, LANES)
    pieces = swap_lane_groups([taps[:, m] for m in range(4)])
    for k in range(4):
        filter_ref[:, 8 * k : 8 * k + 8, :] = pieces[k]

    def put_twisted(at, target, real, imag):
        cosine, sine = cosine_ref[at], sine_ref[at]
        twisted_ref[at, target, 0:LANES] = (real * cosine + imag * sine).astype(BF16)
        twisted_ref[at, target, LANES : 2 * LANES] = (imag * cosine - real * sine).astype(BF16)

    def first_section(left, right, row):
        def parity_rows(parity):
            sides = [
                side.reshape(quarter, 2, PACK, LANES)[:, parity].reshape(quarter * PACK, LANES)
                for side in (left, right)
            ]
            return jnp.dot(
                first_ref[parity], jnp.concatenate(sides, axis=1), preferred_element_type=F32
            )

        even, odd = parity_rows(0), parity_rows(1)
        for side in range(2):
            lanes = slice(LANES * side, LANES * (side + 1))
            target = slice(row + PACK * side, row + PACK * side + PACK)
            even_0, odd_0 = even[0:PACK, lanes], odd[0:PACK, lanes]
            twisted_ref[0, target, 0:LANES] = (even_0 + odd_0).astype(BF16)
            twisted_ref[0, target, LANES : 2 * LANES] = jnp.zeros((PACK, LANES), BF16)
            part = even_0 - odd_0
            twisted_ref[1, target, 0:LANES] = (part * cosine_ref[1]).astype(BF16)
            twisted_ref[1, target, LANES : 2 * LANES] = (-part * sine_ref[1]).astype(BF16)
            put_twisted(half, target, even[PACK : 2 * PACK, lanes], odd[PACK : 2 * PACK, lanes])
            for u in range(1, quarter):
                at_r = slice(2 * u * PACK, (2 * u + 1) * PACK)
                at_i = slice((2 * u + 1) * PACK, (2 * u + 2) * PACK)
                even_r, even_i = even[at_r, lanes], even[at_i, lanes]
                odd_r, odd_i = odd[at_r, lanes], odd[at_i, lanes]
                put_twisted(2 * u, target, even_r + odd_r, even_i + odd_i)
                put_twisted(2 * u + 1, target, even_r - odd_r, odd_i - even_i)

    def places_of(t):
        member = t % 4
        column = (t // 4) * half
        return slice(member * half, member * half + half), column

    for t in range(8):
        places, column = places_of(t)
        left = data_ref[places, column : column + PACK, :]
        right = data_ref[places, column + PACK : column + 2 * PACK, :]
        first_section(left, right, t * half)
    first_section(
        filter_ref[:, 0:PACK, :].astype(BF16), filter_ref[:, PACK : 2 * PACK, :].astype(BF16), 256
    )

    def products(spec):
        filter_r, filter_i = spec[256:288, 0:LANES], spec[256:288, LANES:]
        conv_r, conv_i, back_r, back_i = [], [], [], []
        taps_r = taps_i = None
        for d in range(4):
            at = slice(32 * d, 32 * d + 32)
            value_r, value_i = spec[at, 0:LANES], spec[at, LANES:]
            at = slice(128 + 32 * d, 128 + 32 * d + 32)
            grad_r, grad_i = spec[at, 0:LANES], spec[at, LANES:]
            conv_r.append((value_r * filter_r - value_i * filter_i).astype(BF16))
            conv_i.append((value_r * filter_i + value_i * filter_r).astype(BF16))
            back_r.append((grad_r * filter_r + grad_i * filter_i).astype(BF16))
            back_i.append((grad_i * filter_r - grad_r * filter_i).astype(BF16))
            part_r = grad_r * value_r + grad_i * value_i
            part_i = grad_i * value_r - grad_r * value_i
            taps_r = part_r if d == 0 else taps_r + part_r
            taps_i = part_i if d == 0 else taps_i + part_i
        real = jnp.concatenate(conv_r + back_r + [taps_r.astype(BF16)], axis=0)
        imag = jnp.concatenate(conv_i + back_i + [taps_i.astype(BF16)], axis=0)
        return jnp.concatenate([real, imag], axis=1)

    def spectra(start, count):
        block = twisted_ref[start : start + count].reshape(count * rows, 2 * LANES)
        spec = jnp.dot(block, forward_ref[...], preferred_element_type=F32)
        mixed = jnp.concatenate(
            [products(spec[rows * j : rows * (j + 1)]) for j in range(count)], axis=0
        )
        mixture = jnp.dot(mixed, inverse_ref[...], preferred_element_type=F32)
        results = []
        for j in range(count):
            at = slice(rows * j, rows * (j + 1))
            first, second = mixture[at, 0:LANES], mixture[at, LANES:]
            cosine, sine = cosine_ref[start + j], sine_ref[start + j]
            results.append((first * cosine - second * sine, second * cosine + first * sine))
        return results

    ((middle_r, middle_i),) = spectra(half, 1)
    mixed_ref[0, 1] = middle_r.astype(BF16)
    mixed_ref[1, 1] = middle_i.astype(BF16)
    for u in range(quarter):
        (low_r, low_i), (high_r, high_i) = spectra(2 * u, 2)
        mixed_ref[0, 2 * u] = (low_r + high_r).astype(BF16)
        mixed_ref[1, 2 * u] = (low_r - high_r).astype(BF16)
        if u > 0:
            mixed_ref[0, 2 * u + 1] = (low_i - high_i).astype(BF16)
            mixed_ref[1, 2 * u + 1] = (low_i + high_i).astype(BF16)

    def last_section(row):
        results = []
        for parity in range(2):
            sides = [
                mixed_ref[parity, :, row + PACK * side : row + PACK * side + PACK, :].reshape(half * PACK, LANES)
                for side in range(2)
            ]
            part = jnp.dot(
                last_ref[parity], jnp.concatenate(sides, axis=1), preferred_element_type=F32
            )
            results.append(part.reshape(quarter, PACK, 2 * LANES))
        whole = jnp.stack(results, axis=1).reshape(half, PACK, 2 * LANES)
        return whole[:, :, 0:LANES], whole[:, :, LANES:]

    left, right = last_section(256)
    filter_ref[:, 0:PACK, :] = left
    filter_ref[:, PACK : 2 * PACK, :] = right
    pieces = swap_lane_groups([filter_ref[:, 8 * k : 8 * k + 8, :] for k in range(4)])
    stacked = jnp.stack(pieces, axis=1).reshape(4 * half, 8, LANES)
    out_ref[:, 64:72, :] = stacked.astype(BF16)
    for t in range(8):
        places, column = places_of(t)
        left, right = last_section(t * half)
        out_ref[places, column : column + PACK, :] = left.astype(BF16)
        out_ref[places, column + PACK : column + 2 * PACK, :] = right.astype(BF16)


def convolve(received, tables):
    whole = pl.BlockSpec(memory_space=pltpu.VMEM)
    return pl.pallas_call(
        conv_kernel,
        in_specs=[whole] * 7,
        out_specs=whole,
        out_shape=jax.ShapeDtypeStruct(received.shape, BF16),
        scratch_shapes=[
            pltpu.VMEM((32, 32, LANES), F32),
            pltpu.VMEM((33, 288, 2 * LANES), BF16),
            pltpu.VMEM((2, 32, 288, LANES), BF16),
        ],
        compiler_params=pltpu.CompilerParams(vmem_limit_bytes=CONV_LIMIT),
        name="convolve",
    )(received, *tables)


def exchange(blocks):
    return lax.all_to_all(blocks, ("dp", "ctx"), split_axis=0, concat_axis=0, tiled=True)


def on_device(tables, gate_input, values, cotangent, filter_taps):
    received = exchange(pack(gate_input, values, cotangent, filter_taps))
    returned = exchange(convolve(received, tables))
    return unpack(gate_input, cotangent, returned)


def solution(mesh):
    tables = dft_tables(64)
    specs = (
        P("dp", "ctx", None),
        P("dp", "ctx", None),
        P("dp", "ctx", None),
        P(("dp", "ctx"), None),
    )

    def program(gate_input, values, cotangent, filter_taps):
        body = functools.partial(on_device, tables)
        return jax.shard_map(
            lambda *args: tuple(body(*args)), mesh=mesh, in_specs=specs, out_specs=specs, check_vma=False
        )(*[in_place(x) for x in (gate_input, values, cotangent, filter_taps)])

    return program
```

time: 111 us -> 96.5 us (0.87)
  Pallas kernels: 23.1 us -> 13.6 us
  local copies, waits for them, and re-layouts: 4.76 us -> 0.04 us
    pallas_call x3, Pallas kernels: 23.1 us -> 13.6 us  [the longest x1 6.88 us: convolve(): pl.pallas_call(conv_kernel, in_specs=[whole] * 7, out_specs=whole, out_sh...]
    unnamed x24 -> x12, local copies, waits for them, and re-layouts: 4.76 us -> 0.04 us
where the time goes in v1:
time: 96.5 us; the launch traced here: 96.3 us
  blocking collectives  81.9 us (85%)
  Pallas kernels  13.6 us (14%)
    all_to_all x2, blocking collectives, exchange(): lax.all_to_all(blocks, ('dp', 'ctx'), split_axis=0, concat_axis=0, tiled=...  81.9 us
    pallas_call x1, Pallas kernels, convolve(): pl.pallas_call(conv_kernel, in_specs=[whole] * 7, out_specs=whole, out_sh...  6.88 us
    pallas_call x1, Pallas kernels, unpack(): pl.pallas_call(unpack_kernel, in_specs=[outside, outside, within], out_sp...  3.63 us
    pallas_call x1, Pallas kernels, pack(): pl.pallas_call(pack_kernel, in_specs=[anywhere] * 4, out_specs=pl.BlockSp...  3.05 us

profile of v1, /device:TPU:1, one launch (start us, length us, event | category | flops | bytes accessed | tf_op | source)
XLA Modules:
  0.0 96.3 jit_solution(12041457491284572881)
XLA Ops:
  0.6 3.1 %pack.1 = bf16[128,72,128]{2,1,0:T(8,128)(2,1)S(1)} custom-call(bf16[1,128,4096]{2,1,0:T(8,128)(2,1)} %gate_any.3, bf16[1,128,4096]{2,1,0:T(8,128)(2,1)} %values_any.1, bf16[1,128,4096]{2,1,0:T(8,128)(2,1)} %cotangent_any.3, f32[32,4096]{1,0:T(8,128)} %taps_any.1), custom_call_target="tpu_custom_call" | custom-call | tf_op jit(solution)/shard_map/pack/pallas_call | solution.py:135
  3.7 0.0 copy-start
  3.7 0.0 copy-start.1
  3.7 0.0 copy-start.2
  3.7 0.0 copy-start.3
  3.7 0.0 copy-start.4
  3.8 0.0 copy-start.5
  3.8 44.7 %all_to_all.10.data_ref = bf16[128,72,128]{2,1,0:T(8,128)(2,1)S(1)} all-to-all(bf16[128,72,128]{2,1,0:T(8,128)(2,1)S(1)} %pack.1), channel_id=1, replica_groups=mesh['dp'=4,'ctx'=32] {'dp','ctx'}, dimensions={0} | all-to-all | bytes 4718592 | tf_op jit(solution)/shard_map/all_to_all | solution.py:391
  48.5 0.0 copy-done
  48.5 0.0 copy-done.1
  48.5 0.0 copy-done.2
  48.5 0.0 copy-done.3
  48.5 0.0 copy-done.4
  48.5 0.0 copy-done.5
  48.5 6.9 %convolve.1 = bf16[128,72,128]{2,1,0:T(8,128)(2,1)S(1)} custom-call(bf16[128,72,128]{2,1,0:T(8,128)(2,1)S(1)} %all_to_all.10.data_ref, bf16[2,512,256]{2,1,0:T(8,128)(2,1)S(1)} %copy-done.1, bf16[2,256,512]{2,1,0:T(8,128)(2,1)S(1)} %copy-done, f32[33,1,128]{2,1,0:T(1,128)S(1)} %copy-done.5, f32[33,1,128]{2,1,0:T(1,128)S(1)} %copy-done.4, ...), custom_call_target="tpu_custom_call" | custom-call | tf_op jit(solution)/shard_map/convolve/pallas_call | solution.py:375
  55.4 37.2 %all_to_all.11.packed_ref = bf16[128,72,128]{2,1,0:T(8,128)(2,1)S(1)} all-to-all(bf16[128,72,128]{2,1,0:T(8,128)(2,1)S(1)} %convolve.1), channel_id=1, replica_groups=mesh['dp'=4,'ctx'=32] {'dp','ctx'}, dimensions={0} | all-to-all | bytes 4718592 | tf_op jit(solution)/shard_map/all_to_all | solution.py:391
  92.6 3.6 %unpack.1 = (bf16[1,128,4096]{2,1,0:T(8,128)(2,1)}, bf16[1,128,4096]{2,1,0:T(8,128)(2,1)}, bf16[1,128,4096]{2,1,0:T(8,128)(2,1)}, f32[32,4096]{1,0:T(8,128)}) custom-call(bf16[1,128,4096]{2,1,0:T(8,128)(2,1)} %gate_any.3, bf16[1,128,4096]{2,1,0:T(8,128)(2,1)} %cotangent_any.3, bf16[128,72,128]{2,1,0:T(8,128)(2,1)S(1)} %all_to_all.11.packed_ref), custom_call_target="tpu_custom_call" | custom-call | tf_op jit(solution)/shard_map/unpack/pallas_call | solution.py:218
Async XLA Ops:
  3.7 44.8 %copy-start = (bf16[2,256,512]{2,1,0:T(8,128)(2,1)S(1)}, bf16[2,256,512]{2,1,0:T(8,128)(2,1)}, u32[]{:S(2)}) copy-start(bf16[2,256,512]{2,1,0:T(8,128)(2,1)} %constant.13.clone.last_ref) | copy-start | bytes 1572868
  3.7 44.8 %copy-start.1 = (bf16[2,512,256]{2,1,0:T(8,128)(2,1)S(1)}, bf16[2,512,256]{2,1,0:T(8,128)(2,1)}, u32[]{:S(2)}) copy-start(bf16[2,512,256]{2,1,0:T(8,128)(2,1)} %constant.12.clone.first_ref) | copy-start | bytes 1572868
  3.7 44.8 %copy-start.2 = (bf16[256,256]{1,0:T(8,128)(2,1)S(1)}, bf16[256,256]{1,0:T(8,128)(2,1)}, u32[]{:S(2)}) copy-start(bf16[256,256]{1,0:T(8,128)(2,1)} %constant.17.clone.inverse_ref) | copy-start | bytes 393220
  3.7 44.8 %copy-start.3 = (bf16[256,256]{1,0:T(8,128)(2,1)S(1)}, bf16[256,256]{1,0:T(8,128)(2,1)}, u32[]{:S(2)}) copy-start(bf16[256,256]{1,0:T(8,128)(2,1)} %constant.16.clone.forward_ref) | copy-start | bytes 393220
  3.7 44.8 %copy-start.4 = (f32[33,1,128]{2,1,0:T(1,128)S(1)}, f32[33,1,128]{2,1,0:T(1,128)}, u32[]{:S(2)}) copy-start(f32[33,1,128]{2,1,0:T(1,128)} %constant.15.clone.sine_ref) | copy-start | bytes 50692
  3.8 44.8 %copy-start.5 = (f32[33,1,128]{2,1,0:T(1,128)S(1)}, f32[33,1,128]{2,1,0:T(1,128)}, u32[]{:S(2)}) copy-start(f32[33,1,128]{2,1,0:T(1,128)} %constant.14.clone.cosine_ref) | copy-start | bytes 50692

commit v2 on v1

--- a/solution.py
+++ b/solution.py
@@ -12,6 +12,8 @@
 
 LANES = 128
 PACK = 16
+PACK_CHUNKS = 4
+UNPACK_CHUNKS = 4
 PACK_LIMIT = 16 * 1024 * 1024
 CONV_LIMIT = 32 * 1024 * 1024
 BF16 = jnp.bfloat16
@@ -81,8 +83,8 @@
 
 
 def pack_kernel(
-    gate_any, values_any, cotangent_any, taps_any, packed_ref,
-    gate_ref, values_ref, cotangent_ref, taps_ref, arrived,
+    gate_any, values_any, cotangent_any, taps_any, packed_ref, gate_ref, cotangent_ref,
+    values_ref, taps_ref, arrived,
 ):
     pairs = (
         (values_any, values_ref),
@@ -130,16 +132,18 @@
 
 def pack(gate_input, values, cotangent, filter_taps):
     channels = values.shape[2]
-    chunks = 4
+    chunks = PACK_CHUNKS
     anywhere = pl.BlockSpec(memory_space=pltpu.HBM)
     return pl.pallas_call(
         pack_kernel,
         in_specs=[anywhere] * 4,
-        out_specs=pl.BlockSpec(memory_space=pltpu.VMEM),
-        out_shape=jax.ShapeDtypeStruct((channels // 32, 72, LANES), BF16),
+        out_specs=[pl.BlockSpec(memory_space=pltpu.VMEM)] * 3,
+        out_shape=[
+            jax.ShapeDtypeStruct((channels // 32, 72, LANES), BF16),
+            jax.ShapeDtypeStruct((LANES, channels), BF16),
+            jax.ShapeDtypeStruct((LANES, channels), BF16),
+        ],
         scratch_shapes=[
-            pltpu.VMEM((LANES, channels), BF16),
-            pltpu.VMEM((LANES, channels), BF16),
             pltpu.VMEM((LANES, channels), BF16),
             pltpu.VMEM((32, channels), F32),
             pltpu.SemaphoreType.DMA((4, chunks)),
@@ -150,8 +154,8 @@
 
 
 def unpack_kernel(
-    gate_any, cotangent_any, packed_ref, output_any, gate_grad_any, values_grad_any, taps_any,
-    gate_ref, cotangent_ref, output_ref, gate_grad_ref, values_grad_ref, taps_ref, arrived, left,
+    gate_ref, cotangent_ref, packed_ref, output_any, gate_grad_any, values_grad_any, taps_any,
+    output_ref, gate_grad_ref, values_grad_ref, taps_ref, left,
 ):
     pairs = (
         (values_grad_ref, values_grad_any),
@@ -171,19 +175,16 @@
             return pltpu.make_async_copy(source.at[:, at], target.at[:, at], left.at[m, n])
         return pltpu.make_async_copy(source.at[:, at], target.at[0, :, at], left.at[m, n])
 
-    def fetch(n, m):
-        at = slice(n * columns, (n + 1) * columns)
-        source, target = ((gate_any, gate_ref), (cotangent_any, cotangent_ref))[m]
-        return pltpu.make_async_copy(source.at[0, :, at], target.at[:, at], arrived.at[m, n])
-
-    for n in range(chunks):
-        for m in range(2):
-            fetch(n, m).start()
     for n in range(chunks):
         at = slice(n * columns, (n + 1) * columns)
         of = slice(n * peers, (n + 1) * peers)
         values_grad_ref[:, at] = packed_ref[of, per_peer : 2 * per_peer, :].reshape(columns, LANES).T
         copy(n, 0).start()
+        conv = packed_ref[of, 0:per_peer, :].reshape(columns, LANES).T.astype(F32)
+        output_ref[:, at] = (gate_ref[:, at].astype(F32) * conv).astype(BF16)
+        copy(n, 1).start()
+        gate_grad_ref[:, at] = (cotangent_ref[:, at].astype(F32) * conv).astype(BF16)
+        copy(n, 2).start()
         taps = packed_ref[of, 2 * per_peer : 2 * per_peer + 8, :].astype(F32)
         for block in range(columns // 512):
             pieces = swap_lane_groups(
@@ -195,44 +196,31 @@
                 taps_ref[:, start : start + LANES] = stacked[32 * i : 32 * i + 32, :]
         copy(n, 3).start()
     for n in range(chunks):
-        at = slice(n * columns, (n + 1) * columns)
-        of = slice(n * peers, (n + 1) * peers)
-        conv = packed_ref[of, 0:per_peer, :].reshape(columns, LANES).T.astype(F32)
-        fetch(n, 0).wait()
-        output_ref[:, at] = (gate_ref[:, at].astype(F32) * conv).astype(BF16)
-        copy(n, 1).start()
-        fetch(n, 1).wait()
-        gate_grad_ref[:, at] = (cotangent_ref[:, at].astype(F32) * conv).astype(BF16)
-        copy(n, 2).start()
-    for n in range(chunks):
         for m in range(4):
             copy(n, m).wait()
 
 
 def unpack(gate_input, cotangent, packed):
-    channels = gate_input.shape[2]
-    chunks = 4
+    channels = gate_input.shape[1]
+    chunks = UNPACK_CHUNKS
     within = pl.BlockSpec(memory_space=pltpu.VMEM)
     outside = pl.BlockSpec(memory_space=pltpu.HBM)
-    wide_shape = jax.ShapeDtypeStruct(gate_input.shape, BF16)
+    wide_shape = jax.ShapeDtypeStruct((1, LANES, channels), BF16)
     return pl.pallas_call(
         unpack_kernel,
-        in_specs=[outside, outside, within],
+        in_specs=[within] * 3,
         out_specs=[outside] * 4,
         out_shape=[wide_shape, wide_shape, wide_shape, jax.ShapeDtypeStruct((32, channels), F32)],
         scratch_shapes=[
             pltpu.VMEM((LANES, channels), BF16),
             pltpu.VMEM((LANES, channels), BF16),
             pltpu.VMEM((LANES, channels), BF16),
-            pltpu.VMEM((LANES, channels), BF16),
-            pltpu.VMEM((LANES, channels), BF16),
             pltpu.VMEM((32, channels), F32),
-            pltpu.SemaphoreType.DMA((2, chunks)),
             pltpu.SemaphoreType.DMA((4, chunks)),
         ],
         compiler_params=pltpu.CompilerParams(vmem_limit_bytes=PACK_LIMIT),
         name="unpack",
-    )(in_place(gate_input), in_place(cotangent), packed)
+    )(gate_input, cotangent, packed)
 
 
 def conv_kernel(
@@ -243,8 +231,10 @@
     quarter = 16
     rows = 288
 
-    taps = data_ref[:, 64:72, :].astype(F32).reshape(half, 4, 8, LANES)
-    pieces = swap_lane_groups([taps[:, m] for m in range(4)])
+    taps = data_ref[:, :, 64:72, :].astype(F32).reshape(8, 4, 4, 8, LANES)
+    pieces = swap_lane_groups(
+        [jnp.concatenate([taps[:, m, d] for d in range(4)], axis=0) for m in range(4)]
+    )
     for k in range(4):
         filter_ref[:, 8 * k : 8 * k + 8, :] = pieces[k]
 
@@ -282,15 +272,10 @@
                 put_twisted(2 * u, target, even_r + odd_r, even_i + odd_i)
                 put_twisted(2 * u + 1, target, even_r - odd_r, odd_i - even_i)
 
-    def places_of(t):
-        member = t % 4
+    for t in range(8):
         column = (t // 4) * half
-        return slice(member * half, member * half + half), column
-
-    for t in range(8):
-        places, column = places_of(t)
-        left = data_ref[places, column : column + PACK, :]
-        right = data_ref[places, column + PACK : column + 2 * PACK, :]
+        left = data_ref[:, t % 4, column : column + PACK, :]
+        right = data_ref[:, t % 4, column + PACK : column + 2 * PACK, :]
         first_section(left, right, t * half)
     first_section(
         filter_ref[:, 0:PACK, :].astype(BF16), filter_ref[:, PACK : 2 * PACK, :].astype(BF16), 256
@@ -361,13 +346,16 @@
     filter_ref[:, 0:PACK, :] = left
     filter_ref[:, PACK : 2 * PACK, :] = right
     pieces = swap_lane_groups([filter_ref[:, 8 * k : 8 * k + 8, :] for k in range(4)])
-    stacked = jnp.stack(pieces, axis=1).reshape(4 * half, 8, LANES)
-    out_ref[:, 64:72, :] = stacked.astype(BF16)
+    for m in range(4):
+        for d in range(4):
+            part = pieces[m][8 * d : 8 * d + 8].astype(BF16)
+            for high in range(8):
+                out_ref[4 * high + m, d, 64:72, :] = part[high]
     for t in range(8):
-        places, column = places_of(t)
+        column = (t // 4) * half
         left, right = last_section(t * half)
-        out_ref[places, column : column + PACK, :] = left.astype(BF16)
-        out_ref[places, column + PACK : column + 2 * PACK, :] = right.astype(BF16)
+        out_ref[:, t % 4, column : column + PACK, :] = left.astype(BF16)
+        out_ref[:, t % 4, column + PACK : column + 2 * PACK, :] = right.astype(BF16)
 
 
 def convolve(received, tables):
@@ -388,13 +376,15 @@
 
 
 def exchange(blocks):
-    return lax.all_to_all(blocks, ("dp", "ctx"), split_axis=0, concat_axis=0, tiled=True)
+    return lax.all_to_all(blocks, ("ctx", "dp"), split_axis=0, concat_axis=0, tiled=True)
 
 
 def on_device(tables, gate_input, values, cotangent, filter_taps):
-    received = exchange(pack(gate_input, values, cotangent, filter_taps))
-    returned = exchange(convolve(received, tables))
-    return unpack(gate_input, cotangent, returned)
+    packed, gate_held, cotangent_held = pack(gate_input, values, cotangent, filter_taps)
+    by_member = (lax.axis_size("ctx"), lax.axis_size("dp")) + packed.shape[1:]
+    results = convolve(exchange(packed).reshape(by_member), tables)
+    returned = exchange(results.reshape(packed.shape))
+    return unpack(gate_held, cotangent_held, returned)
 
 
 def solution(mesh):

time: 96.5 us -> 94.2 us (0.976)
  Pallas kernels: 13.6 us -> 12.3 us
    pallas_call x2, Pallas kernels: 6.69 us -> 5.38 us  [the longest x1 3.05 us: pack(): pl.pallas_call(pack_kernel, in_specs=[anywhere] * 4, out_specs=[pl.BlockS...]
where the time goes in v2:
time: 94.2 us; the launch traced here: 94 us
  blocking collectives  81 us (86%)
  Pallas kernels  12.3 us (13%)
    all_to_all x2, blocking collectives, exchange(): lax.all_to_all(blocks, ('ctx', 'dp'), split_axis=0, concat_axis=0, tiled=...  81 us
    pallas_call x1, Pallas kernels, convolve(): pl.pallas_call(conv_kernel, in_specs=[whole] * 7, out_specs=whole, out_sh...  6.88 us
    pallas_call x1, Pallas kernels, pack(): pl.pallas_call(pack_kernel, in_specs=[anywhere] * 4, out_specs=[pl.BlockS...  3.05 us
    pallas_call x1, Pallas kernels, unpack(): pl.pallas_call(unpack_kernel, in_specs=[within] * 3, out_specs=[outside]...  2.33 us

profile of v2, /device:TPU:1, one launch (start us, length us, event | category | flops | bytes accessed | tf_op | source)
XLA Modules:
  0.0 94.0 jit_solution(14666515704324822245)
XLA Ops:
  0.6 3.1 %pack.1 = (bf16[128,72,128]{2,1,0:T(8,128)(2,1)S(1)}, bf16[128,4096]{1,0:T(8,128)(2,1)S(1)}, bf16[128,4096]{1,0:T(8,128)(2,1)S(1)}) custom-call(bf16[1,128,4096]{2,1,0:T(8,128)(2,1)} %gate_any.1, bf16[1,128,4096]{2,1,0:T(8,128)(2,1)} %values_any.1, bf16[1,128,4096]{2,1,0:T(8,128)(2,1)} %cotangent_any.1, f32[32,4096]{1,0:T(8,128)} %taps_any.1), custom_call_target="tpu_custom_call" | custom-call | tf_op jit(solution)/shard_map/pack/pallas_call | solution.py:137
  3.7 0.0 copy-start
  3.7 0.0 copy-start.1
  3.7 0.0 copy-start.2
  3.7 0.0 copy-start.3
  3.7 0.0 copy-start.4
  3.8 0.0 copy-start.5
  3.8 44.0 %all_to_all.10 = bf16[128,72,128]{2,1,0:T(8,128)(2,1)S(1)} all-to-all(bf16[128,72,128]{2,1,0:T(8,128)(2,1)S(1)} %get-tuple-element.9), channel_id=1, replica_groups=mesh['dp'=4,'ctx'=32] {'ctx','dp'}, dimensions={0} | all-to-all | bytes 4718592 | tf_op jit(solution)/shard_map/all_to_all | solution.py:379
  47.8 0.0 copy-done
  47.8 0.0 copy-done.1
  47.8 0.0 copy-done.2
  47.8 0.0 copy-done.3
  47.8 0.0 copy-done.4
  47.8 0.0 copy-done.5
  47.8 6.9 %convolve.1 = bf16[32,4,72,128]{3,2,1,0:T(8,128)(2,1)S(1)} custom-call(bf16[32,4,72,128]{3,2,1,0:T(8,128)(2,1)S(1)} %bitcast.2, bf16[2,512,256]{2,1,0:T(8,128)(2,1)S(1)} %copy-done.1, bf16[2,256,512]{2,1,0:T(8,128)(2,1)S(1)} %copy-done, f32[33,1,128]{2,1,0:T(1,128)S(1)} %copy-done.5, f32[33,1,128]{2,1,0:T(1,128)S(1)} %copy-done.4, ...), custom_call_target="tpu_custom_call" | custom-call | tf_op jit(solution)/shard_map/convolve/pallas_call | solution.py:363
  54.7 37.0 %all_to_all.11.packed_ref = bf16[128,72,128]{2,1,0:T(8,128)(2,1)S(1)} all-to-all(bf16[128,72,128]{2,1,0:T(8,128)(2,1)S(1)} %bitcast.3), channel_id=1, replica_groups=mesh['dp'=4,'ctx'=32] {'ctx','dp'}, dimensions={0} | all-to-all | bytes 4718592 | tf_op jit(solution)/shard_map/all_to_all | solution.py:379
  91.7 2.3 %unpack.1 = (bf16[1,128,4096]{2,1,0:T(8,128)(2,1)}, bf16[1,128,4096]{2,1,0:T(8,128)(2,1)}, bf16[1,128,4096]{2,1,0:T(8,128)(2,1)}, f32[32,4096]{1,0:T(8,128)}) custom-call(bf16[128,4096]{1,0:T(8,128)(2,1)S(1)} %get-tuple-element.7.gate_ref, bf16[128,4096]{1,0:T(8,128)(2,1)S(1)} %get-tuple-element.8.cotangent_ref, bf16[128,72,128]{2,1,0:T(8,128)(2,1)S(1)} %all_to_all.11.packed_ref), custom_call_target="tpu_custom_call" | custom-call | tf_op jit(solution)/shard_map/unpack/pallas_call | solution.py:209
Async XLA Ops:
  3.7 44.1 %copy-start = (bf16[2,256,512]{2,1,0:T(8,128)(2,1)S(1)}, bf16[2,256,512]{2,1,0:T(8,128)(2,1)}, u32[]{:S(2)}) copy-start(bf16[2,256,512]{2,1,0:T(8,128)(2,1)} %constant.13.clone.last_ref) | copy-start | bytes 1572868
  3.7 44.1 %copy-start.1 = (bf16[2,512,256]{2,1,0:T(8,128)(2,1)S(1)}, bf16[2,512,256]{2,1,0:T(8,128)(2,1)}, u32[]{:S(2)}) copy-start(bf16[2,512,256]{2,1,0:T(8,128)(2,1)} %constant.12.clone.first_ref) | copy-start | bytes 1572868
  3.7 44.1 %copy-start.2 = (bf16[256,256]{1,0:T(8,128)(2,1)S(1)}, bf16[256,256]{1,0:T(8,128)(2,1)}, u32[]{:S(2)}) copy-start(bf16[256,256]{1,0:T(8,128)(2,1)} %constant.17.clone.inverse_ref) | copy-start | bytes 393220
  3.7 44.1 %copy-start.3 = (bf16[256,256]{1,0:T(8,128)(2,1)S(1)}, bf16[256,256]{1,0:T(8,128)(2,1)}, u32[]{:S(2)}) copy-start(bf16[256,256]{1,0:T(8,128)(2,1)} %constant.16.clone.forward_ref) | copy-start | bytes 393220
  3.7 44.1 %copy-start.4 = (f32[33,1,128]{2,1,0:T(1,128)S(1)}, f32[33,1,128]{2,1,0:T(1,128)}, u32[]{:S(2)}) copy-start(f32[33,1,128]{2,1,0:T(1,128)} %constant.15.clone.sine_ref) | copy-start | bytes 50692
  3.8 44.1 %copy-start.5 = (f32[33,1,128]{2,1,0:T(1,128)S(1)}, f32[33,1,128]{2,1,0:T(1,128)}, u32[]{:S(2)}) copy-start(f32[33,1,128]{2,1,0:T(1,128)} %constant.14.clone.cosine_ref) | copy-start | bytes 50692

commit v3 on v2

--- a/solution.py
+++ b/solution.py
@@ -49,18 +49,12 @@
         firsts.append(block_diagonal(base))
         lasts.append(block_diagonal((base * weight).T))
     order = [p for u in range(quarter) for p in (u, half - u)] + [quarter]
-    twist_cosine, twist_sine = angle_tables(np.array(order), np.arange(LANES), freq_len)
-    inner_cosine, inner_sine = angle_tables(np.arange(LANES), np.arange(LANES), LANES)
-    forward = np.block([[inner_cosine, -inner_sine], [inner_sine, inner_cosine]])
-    inverse = np.block([[inner_cosine, inner_sine], [-inner_sine, inner_cosine]])
-    return (
-        np.stack(firsts),
-        np.stack(lasts),
-        twist_cosine[:, None, :],
-        twist_sine[:, None, :],
-        forward.astype(ml_dtypes.bfloat16),
-        inverse.astype(ml_dtypes.bfloat16),
-    )
+    forward = []
+    for p in order:
+        cosine, sine = angle_tables(np.arange(LANES), p + blocks * np.arange(LANES), freq_len)
+        forward.append(np.block([[cosine, -sine], [sine, cosine]]))
+    forward = np.stack(forward).astype(ml_dtypes.bfloat16)
+    return (np.stack(firsts), np.stack(lasts), forward)
 
 
 def swap_lane_groups(pieces):
@@ -224,12 +218,11 @@
 
 
 def conv_kernel(
-    data_ref, first_ref, last_ref, cosine_ref, sine_ref, forward_ref, inverse_ref, out_ref,
-    filter_ref, twisted_ref, mixed_ref,
+    data_ref, first_ref, last_ref, forward_ref, out_ref,
+    filter_ref, signal_ref, mixed_ref,
 ):
     half = 32
     quarter = 16
-    rows = 288
 
     taps = data_ref[:, :, 64:72, :].astype(F32).reshape(8, 4, 4, 8, LANES)
     pieces = swap_lane_groups(
@@ -238,10 +231,9 @@
     for k in range(4):
         filter_ref[:, 8 * k : 8 * k + 8, :] = pieces[k]
 
-    def put_twisted(at, target, real, imag):
-        cosine, sine = cosine_ref[at], sine_ref[at]
-        twisted_ref[at, target, 0:LANES] = (real * cosine + imag * sine).astype(BF16)
-        twisted_ref[at, target, LANES : 2 * LANES] = (imag * cosine - real * sine).astype(BF16)
+    def put(at, target, real, imag):
+        signal_ref[at, target, 0:LANES] = real.astype(BF16)
+        signal_ref[at, target, LANES : 2 * LANES] = imag.astype(BF16)
 
     def first_section(left, right, row):
         def parity_rows(parity):
@@ -258,19 +250,17 @@
             lanes = slice(LANES * side, LANES * (side + 1))
             target = slice(row + PACK * side, row + PACK * side + PACK)
             even_0, odd_0 = even[0:PACK, lanes], odd[0:PACK, lanes]
-            twisted_ref[0, target, 0:LANES] = (even_0 + odd_0).astype(BF16)
-            twisted_ref[0, target, LANES : 2 * LANES] = jnp.zeros((PACK, LANES), BF16)
-            part = even_0 - odd_0
-            twisted_ref[1, target, 0:LANES] = (part * cosine_ref[1]).astype(BF16)
-            twisted_ref[1, target, LANES : 2 * LANES] = (-part * sine_ref[1]).astype(BF16)
-            put_twisted(half, target, even[PACK : 2 * PACK, lanes], odd[PACK : 2 * PACK, lanes])
+            nothing = jnp.zeros((PACK, LANES), F32)
+            put(0, target, even_0 + odd_0, nothing)
+            put(1, target, even_0 - odd_0, nothing)
+            put(half, target, even[PACK : 2 * PACK, lanes], odd[PACK : 2 * PACK, lanes])
             for u in range(1, quarter):
                 at_r = slice(2 * u * PACK, (2 * u + 1) * PACK)
                 at_i = slice((2 * u + 1) * PACK, (2 * u + 2) * PACK)
                 even_r, even_i = even[at_r, lanes], even[at_i, lanes]
                 odd_r, odd_i = odd[at_r, lanes], odd[at_i, lanes]
-                put_twisted(2 * u, target, even_r + odd_r, even_i + odd_i)
-                put_twisted(2 * u + 1, target, even_r - odd_r, odd_i - even_i)
+                put(2 * u, target, even_r + odd_r, even_i + odd_i)
+                put(2 * u + 1, target, even_r - odd_r, odd_i - even_i)
 
     for t in range(8):
         column = (t // 4) * half
@@ -303,18 +293,16 @@
         return jnp.concatenate([real, imag], axis=1)
 
     def spectra(start, count):
-        block = twisted_ref[start : start + count].reshape(count * rows, 2 * LANES)
-        spec = jnp.dot(block, forward_ref[...], preferred_element_type=F32)
-        mixed = jnp.concatenate(
-            [products(spec[rows * j : rows * (j + 1)]) for j in range(count)], axis=0
-        )
-        mixture = jnp.dot(mixed, inverse_ref[...], preferred_element_type=F32)
         results = []
-        for j in range(count):
-            at = slice(rows * j, rows * (j + 1))
-            first, second = mixture[at, 0:LANES], mixture[at, LANES:]
-            cosine, sine = cosine_ref[start + j], sine_ref[start + j]
-            results.append((first * cosine - second * sine, second * cosine + first * sine))
+        for at in range(start, start + count):
+            spec = jnp.dot(signal_ref[at], forward_ref[at], preferred_element_type=F32)
+            mixture = lax.dot_general(
+                products(spec),
+                forward_ref[at],
+                (((1,), (1,)), ((), ())),
+                preferred_element_type=F32,
+            )
+            results.append((mixture[:, 0:LANES], mixture[:, LANES:]))
         return results
 
     ((middle_r, middle_i),) = spectra(half, 1)
@@ -362,7 +350,7 @@
     whole = pl.BlockSpec(memory_space=pltpu.VMEM)
     return pl.pallas_call(
         conv_kernel,
-        in_specs=[whole] * 7,
+        in_specs=[whole] * 4,
         out_specs=whole,
         out_shape=jax.ShapeDtypeStruct(received.shape, BF16),
         scratch_shapes=[

time: 94.2 us -> 92.8 us (0.985)
  Pallas kernels: 12.3 us -> 11 us
    pallas_call x1, Pallas kernels: 6.88 us -> 5.52 us  [convolve(): pl.pallas_call(conv_kernel, in_specs=[whole] * 4, out_specs=whole, out_sh...]
where the time goes in v3:
time: 92.8 us; the launch traced here: 92.7 us
  blocking collectives  81 us (87%)
  Pallas kernels  11 us (12%)
    all_to_all x2, blocking collectives, exchange(): lax.all_to_all(blocks, ('ctx', 'dp'), split_axis=0, concat_axis=0, tiled=...  81 us
    pallas_call x1, Pallas kernels, convolve(): pl.pallas_call(conv_kernel, in_specs=[whole] * 4, out_specs=whole, out_sh...  5.52 us
    pallas_call x1, Pallas kernels, pack(): pl.pallas_call(pack_kernel, in_specs=[anywhere] * 4, out_specs=[pl.BlockS...  3.14 us
    pallas_call x1, Pallas kernels, unpack(): pl.pallas_call(unpack_kernel, in_specs=[within] * 3, out_specs=[outside]...  2.32 us

profile of v3, /device:TPU:1, one launch (start us, length us, event | category | flops | bytes accessed | tf_op | source)
XLA Modules:
  0.0 92.7 jit_solution(11791817652484167158)
XLA Ops:
  0.6 0.0 copy-start.1
  0.6 0.0 copy-start.2
  0.7 3.1 %pack.1 = (bf16[128,72,128]{2,1,0:T(8,128)(2,1)S(1)}, bf16[128,4096]{1,0:T(8,128)(2,1)S(1)}, bf16[128,4096]{1,0:T(8,128)(2,1)S(1)}) custom-call(bf16[1,128,4096]{2,1,0:T(8,128)(2,1)} %gate_any.1, bf16[1,128,4096]{2,1,0:T(8,128)(2,1)} %values_any.1, bf16[1,128,4096]{2,1,0:T(8,128)(2,1)} %cotangent_any.1, f32[32,4096]{1,0:T(8,128)} %taps_any.1), custom_call_target="tpu_custom_call" | custom-call | tf_op jit(solution)/shard_map/pack/pallas_call | solution.py:131
  3.8 0.0 copy-start
  3.8 44.0 %all_to_all.10 = bf16[128,72,128]{2,1,0:T(8,128)(2,1)S(1)} all-to-all(bf16[128,72,128]{2,1,0:T(8,128)(2,1)S(1)} %get-tuple-element.9), channel_id=1, replica_groups=mesh['dp'=4,'ctx'=32] {'ctx','dp'}, dimensions={0} | all-to-all | bytes 4718592 | tf_op jit(solution)/shard_map/all_to_all | solution.py:367
  47.8 0.0 copy-done.1
  47.8 0.0 copy-done.2
  47.8 0.0 copy-done
  47.8 5.5 %convolve.1 = bf16[32,4,72,128]{3,2,1,0:T(8,128)(2,1)S(1)} custom-call(bf16[32,4,72,128]{3,2,1,0:T(8,128)(2,1)S(1)} %bitcast.2, bf16[2,512,256]{2,1,0:T(8,128)(2,1)S(1)} %copy-done.2, bf16[2,256,512]{2,1,0:T(8,128)(2,1)S(1)} %copy-done.1, bf16[33,256,256]{2,1,0:T(8,128)(2,1)S(1)} %copy-done), custom_call_target="tpu_custom_call" | custom-call | tf_op jit(solution)/shard_map/convolve/pallas_call | solution.py:351
  53.4 37.0 %all_to_all.11.packed_ref = bf16[128,72,128]{2,1,0:T(8,128)(2,1)S(1)} all-to-all(bf16[128,72,128]{2,1,0:T(8,128)(2,1)S(1)} %bitcast.3), channel_id=1, replica_groups=mesh['dp'=4,'ctx'=32] {'ctx','dp'}, dimensions={0} | all-to-all | bytes 4718592 | tf_op jit(solution)/shard_map/all_to_all | solution.py:367
  90.4 2.3 %unpack.1 = (bf16[1,128,4096]{2,1,0:T(8,128)(2,1)}, bf16[1,128,4096]{2,1,0:T(8,128)(2,1)}, bf16[1,128,4096]{2,1,0:T(8,128)(2,1)}, f32[32,4096]{1,0:T(8,128)}) custom-call(bf16[128,4096]{1,0:T(8,128)(2,1)S(1)} %get-tuple-element.7.gate_ref, bf16[128,4096]{1,0:T(8,128)(2,1)S(1)} %get-tuple-element.8.cotangent_ref, bf16[128,72,128]{2,1,0:T(8,128)(2,1)S(1)} %all_to_all.11.packed_ref), custom_call_target="tpu_custom_call" | custom-call | tf_op jit(solution)/shard_map/unpack/pallas_call | solution.py:203
Async XLA Ops:
  0.6 47.2 %copy-start.1 = (bf16[2,256,512]{2,1,0:T(8,128)(2,1)S(1)}, bf16[2,256,512]{2,1,0:T(8,128)(2,1)}, u32[]{:S(2)}) copy-start(bf16[2,256,512]{2,1,0:T(8,128)(2,1)} %constant.7.clone.last_ref) | copy-start | bytes 1572868
  0.6 47.2 %copy-start.2 = (bf16[2,512,256]{2,1,0:T(8,128)(2,1)S(1)}, bf16[2,512,256]{2,1,0:T(8,128)(2,1)}, u32[]{:S(2)}) copy-start(bf16[2,512,256]{2,1,0:T(8,128)(2,1)} %constant.6.clone.first_ref) | copy-start | bytes 1572868
  3.8 44.0 %copy-start = (bf16[33,256,256]{2,1,0:T(8,128)(2,1)S(1)}, bf16[33,256,256]{2,1,0:T(8,128)(2,1)}, u32[]{:S(2)}) copy-start(bf16[33,256,256]{2,1,0:T(8,128)(2,1)} %constant.8.clone.forward_ref) | copy-start | bytes 12976132

commit v4 on v3

--- a/solution.py
+++ b/solution.py
@@ -12,7 +12,7 @@
 
 LANES = 128
 PACK = 16
-PACK_CHUNKS = 4
+PACK_CHUNKS = 1
 UNPACK_CHUNKS = 4
 PACK_LIMIT = 16 * 1024 * 1024
 CONV_LIMIT = 32 * 1024 * 1024

time: 92.8 us -> 92.4 us (level)
  no operation moved by 1% of the time
where the time goes in v4:
time: 92.4 us; the launch traced here: 92.3 us
  blocking collectives  81 us (88%)
  Pallas kernels  10.6 us (11%)
    all_to_all x2, blocking collectives, exchange(): lax.all_to_all(blocks, ('ctx', 'dp'), split_axis=0, concat_axis=0, tiled=...  81 us
    pallas_call x1, Pallas kernels, convolve(): pl.pallas_call(conv_kernel, in_specs=[whole] * 4, out_specs=whole, out_sh...  5.52 us
    pallas_call x1, Pallas kernels, pack(): pl.pallas_call(pack_kernel, in_specs=[anywhere] * 4, out_specs=[pl.BlockS...  2.74 us
    pallas_call x1, Pallas kernels, unpack(): pl.pallas_call(unpack_kernel, in_specs=[within] * 3, out_specs=[outside]...  2.32 us

profile of v4, /device:TPU:1, one launch (start us, length us, event | category | flops | bytes accessed | tf_op | source)
XLA Modules:
  0.0 92.3 jit_solution(4284537497909230849)
XLA Ops:
  0.6 0.0 copy-start.1
  0.6 0.0 copy-start.2
  0.7 2.7 %pack.1 = (bf16[128,72,128]{2,1,0:T(8,128)(2,1)S(1)}, bf16[128,4096]{1,0:T(8,128)(2,1)S(1)}, bf16[128,4096]{1,0:T(8,128)(2,1)S(1)}) custom-call(bf16[1,128,4096]{2,1,0:T(8,128)(2,1)} %gate_any.1, bf16[1,128,4096]{2,1,0:T(8,128)(2,1)} %values_any.1, bf16[1,128,4096]{2,1,0:T(8,128)(2,1)} %cotangent_any.1, f32[32,4096]{1,0:T(8,128)} %taps_any.1), custom_call_target="tpu_custom_call" | custom-call | tf_op jit(solution)/shard_map/pack/pallas_call | solution.py:131
  3.4 0.0 copy-start
  3.4 44.0 %all_to_all.10 = bf16[128,72,128]{2,1,0:T(8,128)(2,1)S(1)} all-to-all(bf16[128,72,128]{2,1,0:T(8,128)(2,1)S(1)} %get-tuple-element.9), channel_id=1, replica_groups=mesh['dp'=4,'ctx'=32] {'ctx','dp'}, dimensions={0} | all-to-all | bytes 4718592 | tf_op jit(solution)/shard_map/all_to_all | solution.py:367
  47.4 0.0 copy-done.1
  47.4 0.0 copy-done.2
  47.4 0.0 copy-done
  47.4 5.5 %convolve.1 = bf16[32,4,72,128]{3,2,1,0:T(8,128)(2,1)S(1)} custom-call(bf16[32,4,72,128]{3,2,1,0:T(8,128)(2,1)S(1)} %bitcast.2, bf16[2,512,256]{2,1,0:T(8,128)(2,1)S(1)} %copy-done.2, bf16[2,256,512]{2,1,0:T(8,128)(2,1)S(1)} %copy-done.1, bf16[33,256,256]{2,1,0:T(8,128)(2,1)S(1)} %copy-done), custom_call_target="tpu_custom_call" | custom-call | tf_op jit(solution)/shard_map/convolve/pallas_call | solution.py:351
  53.0 37.0 %all_to_all.11.packed_ref = bf16[128,72,128]{2,1,0:T(8,128)(2,1)S(1)} all-to-all(bf16[128,72,128]{2,1,0:T(8,128)(2,1)S(1)} %bitcast.3), channel_id=1, replica_groups=mesh['dp'=4,'ctx'=32] {'ctx','dp'}, dimensions={0} | all-to-all | bytes 4718592 | tf_op jit(solution)/shard_map/all_to_all | solution.py:367
  89.9 2.3 %unpack.1 = (bf16[1,128,4096]{2,1,0:T(8,128)(2,1)}, bf16[1,128,4096]{2,1,0:T(8,128)(2,1)}, bf16[1,128,4096]{2,1,0:T(8,128)(2,1)}, f32[32,4096]{1,0:T(8,128)}) custom-call(bf16[128,4096]{1,0:T(8,128)(2,1)S(1)} %get-tuple-element.7.gate_ref, bf16[128,4096]{1,0:T(8,128)(2,1)S(1)} %get-tuple-element.8.cotangent_ref, bf16[128,72,128]{2,1,0:T(8,128)(2,1)S(1)} %all_to_all.11.packed_ref), custom_call_target="tpu_custom_call" | custom-call | tf_op jit(solution)/shard_map/unpack/pallas_call | solution.py:203
Async XLA Ops:
  0.6 46.8 %copy-start.1 = (bf16[2,256,512]{2,1,0:T(8,128)(2,1)S(1)}, bf16[2,256,512]{2,1,0:T(8,128)(2,1)}, u32[]{:S(2)}) copy-start(bf16[2,256,512]{2,1,0:T(8,128)(2,1)} %constant.7.clone.last_ref) | copy-start | bytes 1572868
  0.6 46.8 %copy-start.2 = (bf16[2,512,256]{2,1,0:T(8,128)(2,1)S(1)}, bf16[2,512,256]{2,1,0:T(8,128)(2,1)}, u32[]{:S(2)}) copy-start(bf16[2,512,256]{2,1,0:T(8,128)(2,1)} %constant.6.clone.first_ref) | copy-start | bytes 1572868
  3.4 44.0 %copy-start = (bf16[33,256,256]{2,1,0:T(8,128)(2,1)S(1)}, bf16[33,256,256]{2,1,0:T(8,128)(2,1)}, u32[]{:S(2)}) copy-start(bf16[33,256,256]{2,1,0:T(8,128)(2,1)} %constant.8.clone.forward_ref) | copy-start | bytes 12976132

commit v5 on v4

--- a/solution.py
+++ b/solution.py
@@ -28,6 +28,12 @@
 def block_diagonal(table):
     eye = np.eye(PACK, dtype=np.float32)
     return np.kron(table, eye).astype(ml_dtypes.bfloat16)
+
+
+def frequency_order(half):
+    quarter, eighth = half // 2, half // 4
+    quads = [p for u in range(1, eighth) for p in (u, half - u, quarter - u, quarter + u)]
+    return quads + [eighth, half - eighth, 0, half, quarter]
 
 
 def dft_tables(blocks):
@@ -44,11 +50,19 @@
         for p in range(1, quarter):
             base[2 * p] = cosine[p]
             base[2 * p + 1] = -sine[p]
-        weight = np.full((half, 1), 2.0 / freq_len, np.float32)
-        weight[0] = 1.0 / freq_len
         firsts.append(block_diagonal(base))
-        lasts.append(block_diagonal((base * weight).T))
-    order = [p for u in range(quarter) for p in (u, half - u)] + [quarter]
+    eighth = quarter // 2
+    for residue in range(4):
+        places = np.arange(residue, half, 4)
+        cosine, sine = angle_tables(np.arange(eighth + 1), places, blocks)
+        base = np.zeros((quarter, eighth), np.float32)
+        base[0] = 0.5
+        base[1] = sine[eighth] * -1.0 if residue == 2 else cosine[eighth]
+        for p in range(1, eighth):
+            base[2 * p] = cosine[p]
+            base[2 * p + 1] = -sine[p]
+        lasts.append(block_diagonal((base * (2.0 / freq_len)).T))
+    order = frequency_order(half)
     forward = []
     for p in order:
         cosine, sine = angle_tables(np.arange(LANES), p + blocks * np.arange(LANES), freq_len)
@@ -231,7 +245,10 @@
     for k in range(4):
         filter_ref[:, 8 * k : 8 * k + 8, :] = pieces[k]
 
-    def put(at, target, real, imag):
+    place = {p: at for at, p in enumerate(frequency_order(half))}
+
+    def put(p, target, real, imag):
+        at = place[p]
         signal_ref[at, target, 0:LANES] = real.astype(BF16)
         signal_ref[at, target, LANES : 2 * LANES] = imag.astype(BF16)
 
@@ -252,15 +269,15 @@
             even_0, odd_0 = even[0:PACK, lanes], odd[0:PACK, lanes]
             nothing = jnp.zeros((PACK, LANES), F32)
             put(0, target, even_0 + odd_0, nothing)
-            put(1, target, even_0 - odd_0, nothing)
-            put(half, target, even[PACK : 2 * PACK, lanes], odd[PACK : 2 * PACK, lanes])
+            put(half, target, even_0 - odd_0, nothing)
+            put(quarter, target, even[PACK : 2 * PACK, lanes], odd[PACK : 2 * PACK, lanes])
             for u in range(1, quarter):
                 at_r = slice(2 * u * PACK, (2 * u + 1) * PACK)
                 at_i = slice((2 * u + 1) * PACK, (2 * u + 2) * PACK)
                 even_r, even_i = even[at_r, lanes], even[at_i, lanes]
                 odd_r, odd_i = odd[at_r, lanes], odd[at_i, lanes]
-                put(2 * u, target, even_r + odd_r, even_i + odd_i)
-                put(2 * u + 1, target, even_r - odd_r, odd_i - even_i)
+                put(u, target, even_r + odd_r, even_i + odd_i)
+                put(half - u, target, even_r - odd_r, odd_i - even_i)
 
     for t in range(8):
         column = (t // 4) * half
@@ -292,41 +309,51 @@
         imag = jnp.concatenate(conv_i + back_i + [taps_i.astype(BF16)], axis=0)
         return jnp.concatenate([real, imag], axis=1)
 
-    def spectra(start, count):
-        results = []
-        for at in range(start, start + count):
-            spec = jnp.dot(signal_ref[at], forward_ref[at], preferred_element_type=F32)
-            mixture = lax.dot_general(
-                products(spec),
-                forward_ref[at],
-                (((1,), (1,)), ((), ())),
-                preferred_element_type=F32,
-            )
-            results.append((mixture[:, 0:LANES], mixture[:, LANES:]))
-        return results
-
-    ((middle_r, middle_i),) = spectra(half, 1)
-    mixed_ref[0, 1] = middle_r.astype(BF16)
-    mixed_ref[1, 1] = middle_i.astype(BF16)
-    for u in range(quarter):
-        (low_r, low_i), (high_r, high_i) = spectra(2 * u, 2)
-        mixed_ref[0, 2 * u] = (low_r + high_r).astype(BF16)
-        mixed_ref[1, 2 * u] = (low_r - high_r).astype(BF16)
-        if u > 0:
-            mixed_ref[0, 2 * u + 1] = (low_i - high_i).astype(BF16)
-            mixed_ref[1, 2 * u + 1] = (low_i + high_i).astype(BF16)
+    def spectrum(p):
+        at = place[p]
+        spec = jnp.dot(signal_ref[at], forward_ref[at], preferred_element_type=F32)
+        mixture = lax.dot_general(
+            products(spec),
+            forward_ref[at],
+            (((1,), (1,)), ((), ())),
+            preferred_element_type=F32,
+        )
+        return mixture[:, 0:LANES], mixture[:, LANES:]
+
+    def halves(p):
+        (low_r, low_i), (high_r, high_i) = spectrum(p), spectrum(half - p)
+        return low_r + high_r, low_i - high_i, low_r - high_r, low_i + high_i
+
+    def mix(at, *parts):
+        for residue in range(4):
+            mixed_ref[residue, at] = parts[residue].astype(BF16)
+
+    eighth = quarter // 2
+    for u in range(1, eighth):
+        even_r, even_i, odd_r, odd_i = halves(u)
+        other_r, other_i, across_r, across_i = halves(quarter - u)
+        mix(2 * u, even_r + other_r, odd_r - across_i, even_r - other_r, odd_r + across_i)
+        mix(2 * u + 1, even_i - other_i, odd_i - across_r, even_i + other_i, odd_i + across_r)
+    even_r, even_i, odd_r, odd_i = halves(eighth)
+    mix(1, even_r, odd_r - odd_i, even_i, odd_r + odd_i)
+    first, last = spectrum(0)[0], spectrum(half)[0]
+    middle_r, middle_i = spectrum(quarter)
+    even, odd = first + last, first - last
+    mix(0, even + 2.0 * middle_r, odd - 2.0 * middle_i, even - 2.0 * middle_r, odd + 2.0 * middle_i)
 
     def last_section(row):
         results = []
-        for parity in range(2):
+        for residue in range(4):
             sides = [
-                mixed_ref[parity, :, row + PACK * side : row + PACK * side + PACK, :].reshape(half * PACK, LANES)
+                mixed_ref[residue, :, row + PACK * side : row + PACK * side + PACK, :].reshape(
+                    quarter * PACK, LANES
+                )
                 for side in range(2)
             ]
             part = jnp.dot(
-                last_ref[parity], jnp.concatenate(sides, axis=1), preferred_element_type=F32
+                last_ref[residue], jnp.concatenate(sides, axis=1), preferred_element_type=F32
             )
-            results.append(part.reshape(quarter, PACK, 2 * LANES))
+            results.append(part.reshape(eighth, PACK, 2 * LANES))
         whole = jnp.stack(results, axis=1).reshape(half, PACK, 2 * LANES)
         return whole[:, :, 0:LANES], whole[:, :, LANES:]
 
@@ -356,7 +383,7 @@
         scratch_shapes=[
             pltpu.VMEM((32, 32, LANES), F32),
             pltpu.VMEM((33, 288, 2 * LANES), BF16),
-            pltpu.VMEM((2, 32, 288, LANES), BF16),
+            pltpu.VMEM((4, 16, 288, LANES), BF16),
         ],
         compiler_params=pltpu.CompilerParams(vmem_limit_bytes=CONV_LIMIT),
         name="convolve",

time: 92.4 us -> 92.3 us (level)
  no operation moved by 1% of the time
where the time goes in v5:
time: 92.3 us; the launch traced here: 92.1 us
  blocking collectives  81 us (88%)
  Pallas kernels  10.4 us (11%)
    all_to_all x2, blocking collectives, exchange(): lax.all_to_all(blocks, ('ctx', 'dp'), split_axis=0, concat_axis=0, tiled=...  81 us
    pallas_call x1, Pallas kernels, convolve(): pl.pallas_call(conv_kernel, in_specs=[whole] * 4, out_specs=whole, out_sh...  5.4 us
    pallas_call x1, Pallas kernels, pack(): pl.pallas_call(pack_kernel, in_specs=[anywhere] * 4, out_specs=[pl.BlockS...  2.71 us
    pallas_call x1, Pallas kernels, unpack(): pl.pallas_call(unpack_kernel, in_specs=[within] * 3, out_specs=[outside]...  2.32 us

profile of v5, /device:TPU:1, one launch (start us, length us, event | category | flops | bytes accessed | tf_op | source)
XLA Modules:
  0.0 92.1 jit_solution(14714169879167797352)
XLA Ops:
  0.6 0.0 copy-start.1
  0.6 2.7 %pack.1 = (bf16[128,72,128]{2,1,0:T(8,128)(2,1)S(1)}, bf16[128,4096]{1,0:T(8,128)(2,1)S(1)}, bf16[128,4096]{1,0:T(8,128)(2,1)S(1)}) custom-call(bf16[1,128,4096]{2,1,0:T(8,128)(2,1)} %gate_any.1, bf16[1,128,4096]{2,1,0:T(8,128)(2,1)} %values_any.1, bf16[1,128,4096]{2,1,0:T(8,128)(2,1)} %cotangent_any.1, f32[32,4096]{1,0:T(8,128)} %taps_any.1), custom_call_target="tpu_custom_call" | custom-call | tf_op jit(solution)/shard_map/pack/pallas_call | solution.py:145
  3.4 0.0 copy-start
  3.4 0.0 copy-start.2
  3.4 44.0 %all_to_all.10 = bf16[128,72,128]{2,1,0:T(8,128)(2,1)S(1)} all-to-all(bf16[128,72,128]{2,1,0:T(8,128)(2,1)S(1)} %get-tuple-element.9), channel_id=1, replica_groups=mesh['dp'=4,'ctx'=32] {'ctx','dp'}, dimensions={0} | all-to-all | bytes 4718592 | tf_op jit(solution)/shard_map/all_to_all | solution.py:394
  47.4 0.0 copy-done.1
  47.4 0.0 copy-done
  47.4 0.0 copy-done.2
  47.4 5.4 %convolve.1 = bf16[32,4,72,128]{3,2,1,0:T(8,128)(2,1)S(1)} custom-call(bf16[32,4,72,128]{3,2,1,0:T(8,128)(2,1)S(1)} %bitcast.2, bf16[2,512,256]{2,1,0:T(8,128)(2,1)S(1)} %copy-done.1, bf16[4,128,256]{2,1,0:T(8,128)(2,1)S(1)} %copy-done.2, bf16[33,256,256]{2,1,0:T(8,128)(2,1)S(1)} %copy-done), custom_call_target="tpu_custom_call" | custom-call | tf_op jit(solution)/shard_map/convolve/pallas_call | solution.py:378
  52.8 37.0 %all_to_all.11.packed_ref = bf16[128,72,128]{2,1,0:T(8,128)(2,1)S(1)} all-to-all(bf16[128,72,128]{2,1,0:T(8,128)(2,1)S(1)} %bitcast.3), channel_id=1, replica_groups=mesh['dp'=4,'ctx'=32] {'ctx','dp'}, dimensions={0} | all-to-all | bytes 4718592 | tf_op jit(solution)/shard_map/all_to_all | solution.py:394
  89.8 2.3 %unpack.1 = (bf16[1,128,4096]{2,1,0:T(8,128)(2,1)}, bf16[1,128,4096]{2,1,0:T(8,128)(2,1)}, bf16[1,128,4096]{2,1,0:T(8,128)(2,1)}, f32[32,4096]{1,0:T(8,128)}) custom-call(bf16[128,4096]{1,0:T(8,128)(2,1)S(1)} %get-tuple-element.7.gate_ref, bf16[128,4096]{1,0:T(8,128)(2,1)S(1)} %get-tuple-element.8.cotangent_ref, bf16[128,72,128]{2,1,0:T(8,128)(2,1)S(1)} %all_to_all.11.packed_ref), custom_call_target="tpu_custom_call" | custom-call | tf_op jit(solution)/shard_map/unpack/pallas_call | solution.py:217
Async XLA Ops:
  0.6 46.8 %copy-start.1 = (bf16[2,512,256]{2,1,0:T(8,128)(2,1)S(1)}, bf16[2,512,256]{2,1,0:T(8,128)(2,1)}, u32[]{:S(2)}) copy-start(bf16[2,512,256]{2,1,0:T(8,128)(2,1)} %constant.6.clone.first_ref) | copy-start | bytes 1572868
  3.4 44.1 %copy-start = (bf16[33,256,256]{2,1,0:T(8,128)(2,1)S(1)}, bf16[33,256,256]{2,1,0:T(8,128)(2,1)}, u32[]{:S(2)}) copy-start(bf16[33,256,256]{2,1,0:T(8,128)(2,1)} %constant.8.clone.forward_ref) | copy-start | bytes 12976132
  3.4 44.0 %copy-start.2 = (bf16[4,128,256]{2,1,0:T(8,128)(2,1)S(1)}, bf16[4,128,256]{2,1,0:T(8,128)(2,1)}, u32[]{:S(2)}) copy-start(bf16[4,128,256]{2,1,0:T(8,128)(2,1)} %constant.7.clone.last_ref) | copy-start | bytes 786436

commit v6 on v5

--- a/solution.py
+++ b/solution.py
@@ -329,11 +329,6 @@
             mixed_ref[residue, at] = parts[residue].astype(BF16)
 
     eighth = quarter // 2
-    for u in range(1, eighth):
-        even_r, even_i, odd_r, odd_i = halves(u)
-        other_r, other_i, across_r, across_i = halves(quarter - u)
-        mix(2 * u, even_r + other_r, odd_r - across_i, even_r - other_r, odd_r + across_i)
-        mix(2 * u + 1, even_i - other_i, odd_i - across_r, even_i + other_i, odd_i + across_r)
     even_r, even_i, odd_r, odd_i = halves(eighth)
     mix(1, even_r, odd_r - odd_i, even_i, odd_r + odd_i)
     first, last = spectrum(0)[0], spectrum(half)[0]
@@ -341,6 +336,11 @@
     even, odd = first + last, first - last
     mix(0, even + 2.0 * middle_r, odd - 2.0 * middle_i, even - 2.0 * middle_r, odd + 2.0 * middle_i)
 
+    for u in range(1, eighth):
+        even_r, even_i, odd_r, odd_i = halves(u)
+        other_r, other_i, across_r, across_i = halves(quarter - u)
+        mix(2 * u, even_r + other_r, odd_r - across_i, even_r - other_r, odd_r + across_i)
+        mix(2 * u + 1, even_i - other_i, odd_i - across_r, even_i + other_i, odd_i + across_r)
     def last_section(row):
         results = []
         for residue in range(4):

time: 92.3 us -> 92.2 us (level)
  no operation moved by 1% of the time
where the time goes in v6:
time: 92.2 us; the launch traced here: 92 us
  blocking collectives  81 us (88%)
  Pallas kernels  10.4 us (11%)
    all_to_all x2, blocking collectives, exchange(): lax.all_to_all(blocks, ('ctx', 'dp'), split_axis=0, concat_axis=0, tiled=...  81 us
    pallas_call x1, Pallas kernels, convolve(): pl.pallas_call(conv_kernel, in_specs=[whole] * 4, out_specs=whole, out_sh...  5.32 us
    pallas_call x1, Pallas kernels, pack(): pl.pallas_call(pack_kernel, in_specs=[anywhere] * 4, out_specs=[pl.BlockS...  2.71 us
    pallas_call x1, Pallas kernels, unpack(): pl.pallas_call(unpack_kernel, in_specs=[within] * 3, out_specs=[outside]...  2.32 us

profile of v6, /device:TPU:1, one launch (start us, length us, event | category | flops | bytes accessed | tf_op | source)
XLA Modules:
  0.0 92.0 jit_solution(3314977400898713018)
XLA Ops:
  0.6 0.0 copy-start.1
  0.6 2.7 %pack.1 = (bf16[128,72,128]{2,1,0:T(8,128)(2,1)S(1)}, bf16[128,4096]{1,0:T(8,128)(2,1)S(1)}, bf16[128,4096]{1,0:T(8,128)(2,1)S(1)}) custom-call(bf16[1,128,4096]{2,1,0:T(8,128)(2,1)} %gate_any.1, bf16[1,128,4096]{2,1,0:T(8,128)(2,1)} %values_any.1, bf16[1,128,4096]{2,1,0:T(8,128)(2,1)} %cotangent_any.1, f32[32,4096]{1,0:T(8,128)} %taps_any.1), custom_call_target="tpu_custom_call" | custom-call | tf_op jit(solution)/shard_map/pack/pallas_call | solution.py:145
  3.4 0.0 copy-start
  3.4 0.0 copy-start.2
  3.4 44.0 %all_to_all.10 = bf16[128,72,128]{2,1,0:T(8,128)(2,1)S(1)} all-to-all(bf16[128,72,128]{2,1,0:T(8,128)(2,1)S(1)} %get-tuple-element.9), channel_id=1, replica_groups=mesh['dp'=4,'ctx'=32] {'ctx','dp'}, dimensions={0} | all-to-all | bytes 4718592 | tf_op jit(solution)/shard_map/all_to_all | solution.py:394
  47.4 0.0 copy-done.1
  47.4 0.0 copy-done
  47.4 0.0 copy-done.2
  47.4 5.3 %convolve.1 = bf16[32,4,72,128]{3,2,1,0:T(8,128)(2,1)S(1)} custom-call(bf16[32,4,72,128]{3,2,1,0:T(8,128)(2,1)S(1)} %bitcast.2, bf16[2,512,256]{2,1,0:T(8,128)(2,1)S(1)} %copy-done.1, bf16[4,128,256]{2,1,0:T(8,128)(2,1)S(1)} %copy-done.2, bf16[33,256,256]{2,1,0:T(8,128)(2,1)S(1)} %copy-done), custom_call_target="tpu_custom_call" | custom-call | tf_op jit(solution)/shard_map/convolve/pallas_call | solution.py:378
  52.7 37.0 %all_to_all.11.packed_ref = bf16[128,72,128]{2,1,0:T(8,128)(2,1)S(1)} all-to-all(bf16[128,72,128]{2,1,0:T(8,128)(2,1)S(1)} %bitcast.3), channel_id=1, replica_groups=mesh['dp'=4,'ctx'=32] {'ctx','dp'}, dimensions={0} | all-to-all | bytes 4718592 | tf_op jit(solution)/shard_map/all_to_all | solution.py:394
  89.7 2.3 %unpack.1 = (bf16[1,128,4096]{2,1,0:T(8,128)(2,1)}, bf16[1,128,4096]{2,1,0:T(8,128)(2,1)}, bf16[1,128,4096]{2,1,0:T(8,128)(2,1)}, f32[32,4096]{1,0:T(8,128)}) custom-call(bf16[128,4096]{1,0:T(8,128)(2,1)S(1)} %get-tuple-element.7.gate_ref, bf16[128,4096]{1,0:T(8,128)(2,1)S(1)} %get-tuple-element.8.cotangent_ref, bf16[128,72,128]{2,1,0:T(8,128)(2,1)S(1)} %all_to_all.11.packed_ref), custom_call_target="tpu_custom_call" | custom-call | tf_op jit(solution)/shard_map/unpack/pallas_call | solution.py:217
Async XLA Ops:
  0.6 46.8 %copy-start.1 = (bf16[2,512,256]{2,1,0:T(8,128)(2,1)S(1)}, bf16[2,512,256]{2,1,0:T(8,128)(2,1)}, u32[]{:S(2)}) copy-start(bf16[2,512,256]{2,1,0:T(8,128)(2,1)} %constant.6.clone.first_ref) | copy-start | bytes 1572868
  3.4 44.1 %copy-start = (bf16[33,256,256]{2,1,0:T(8,128)(2,1)S(1)}, bf16[33,256,256]{2,1,0:T(8,128)(2,1)}, u32[]{:S(2)}) copy-start(bf16[33,256,256]{2,1,0:T(8,128)(2,1)} %constant.8.clone.forward_ref) | copy-start | bytes 12976132
  3.4 44.0 %copy-start.2 = (bf16[4,128,256]{2,1,0:T(8,128)(2,1)S(1)}, bf16[4,128,256]{2,1,0:T(8,128)(2,1)}, u32[]{:S(2)}) copy-start(bf16[4,128,256]{2,1,0:T(8,128)(2,1)} %constant.7.clone.last_ref) | copy-start | bytes 786436
